TPU v7x, 32 devices: a whole 2x2x4 slice. The times are simulated.
32 devices in a mesh: fsdp: 8 (over z, x), rep: 4 (over y, core).
Axes of the slice: x: 2, y: 2, z: 4, core: 2. Of those that a mesh axis runs over, the one named last changes fastest.
Arguments:
- hidden_in: bfloat16 [16384, 768], P(('fsdp', 'rep')), may hold values from -6 to 6
- cotangent: bfloat16 [16384, 768], P(('fsdp', 'rep')), may hold values from -6 to 6
- lengths: int32 [32], P(('fsdp', 'rep')), may hold values from 1 to 512, as said below
- norm_gain: bfloat16 [768], P('fsdp'), may hold values from 0.5 to 1.5
- in_weight: bfloat16 [768, 3352], P('fsdp'), may hold values from -0.21875 to 0.21875
- conv_weight: bfloat16 [4, 1792], P(None, 'fsdp'), may hold values from -3 to 3
- conv_bias: bfloat16 [1792], P('fsdp'), may hold values from -2 to 2
- step_bias: float32 [24], replicated, may hold values from -6 to -2
- decay_log: float32 [24], replicated, may hold values from 0 to 2.77
- skip_weight: float32 [24], replicated, may hold values from 0.5 to 1.5
- mix_gain: bfloat16 [1536], P('fsdp'), may hold values from 0.5 to 1.5
- out_weight: bfloat16 [1536, 768], P('fsdp'), may hold values from -0.15625 to 0.15625
Outputs:
- block_out: bfloat16 [16384, 768], P(('fsdp', 'rep'))
- grad_in: float32 [16384, 768], P(('fsdp', 'rep'))
- grad_norm_gain: float32 [768], P('fsdp')
- grad_in_weight: float32 [768, 3352], P('fsdp')
- grad_conv_weight: float32 [4, 1792], P(None, 'fsdp')
- grad_conv_bias: float32 [1792], P('fsdp')
- grad_step_bias: float32 [24], replicated
- grad_decay_log: float32 [24], replicated
- grad_skip_weight: float32 [24], replicated
- grad_mix_gain: float32 [1536], P('fsdp')
- grad_out_weight: float32 [1536, 768], P('fsdp')
Inputs may be any that keep to these rules, and one draw needn't show every extreme that they name: lengths[s] is the number of live tokens of sequence s, which fill its first slots; some sequence has 512 live tokens.
All inputs are finite; a program needn't handle non-finite values.
Results may differ from a plain program's by a relative error of at most 0.0068.
Values may be sent and summed in bfloat16 or wider, within the bound.
A program may use at most 192 MiB of HBM per device.

v0:
```python
import functools


import jax
import jax.numpy as jnp
from jax import lax
from jax.experimental import pallas as pl
from jax.experimental.pallas import tpu as pltpu
from jax.sharding import PartitionSpec as P

NH = 24
HD = 64
NS = 128
KCONV = 4
DI = 1536
CONV_CH = 1792
PROJ = 3352
LANES = 128
PAIR = LANES // HD
CUTS = (0, 1152, 2304, PROJ)

EPS = 1e-05
HIGH = lax.Precision.HIGHEST


def pre_norm(rows, gain):
    scale = lax.rsqrt(jnp.mean(rows * rows, axis=-1, keepdims=True) + EPS)
    return rows * scale * gain


def contract(left, right, left_dim, right_dim, precision=None):
    return lax.dot_general(
        left,
        right,
        (((left_dim,), (right_dim,)), ((), ())),
        precision=precision,
        preferred_element_type=jnp.float32,
    )


def column_of(array, head):
    lane = lax.broadcasted_iota(jnp.int32, array.shape, 1)
    return jnp.sum(jnp.where(lane == head, array, 0.0), axis=1, keepdims=True)


def tiles_of(length):
    half = length // 2
    return half, ((0, 0), (1, 0), (1, 1))


def decay_tile(cum_col, cum_row, half, row, col):
    spread = cum_col[row * half : (row + 1) * half] - cum_row[:, col * half : (col + 1) * half]
    if row == col:
        rows = lax.broadcasted_iota(jnp.int32, spread.shape, 0)
        cols = lax.broadcasted_iota(jnp.int32, spread.shape, 1)
        spread = jnp.where(rows >= cols, spread, -jnp.inf)
    return jnp.exp(spread)


def pair_lanes(shape):
    return lax.broadcasted_iota(jnp.int32, shape, 1) // HD


def scan_fwd_kernel(x_ref, dt_ref, cum_ref, cumt_ref, b_ref, c_ref, skip_ref, y_ref, score):
    pair = pl.program_id(0)
    length = x_ref.shape[0]
    half, tiles = tiles_of(length)

    @pl.when(pair == 0)
    def _():
        score[...] = contract(c_ref[...], b_ref[...], 1, 1, HIGH)

    which = pair_lanes(x_ref.shape)
    x = x_ref[...]
    sums = [None, None]
    for sub in range(PAIR):
        head = pair * PAIR + sub
        cum_col = column_of(cum_ref[...], head)
        cum_row = cumt_ref[pl.ds(head, 1), :]
        scaled = jnp.where(which == sub, x * column_of(dt_ref[...], head), 0.0)
        scaled = scaled.astype(jnp.bfloat16)
        for row, col in tiles:
            decay = decay_tile(cum_col, cum_row, half, row, col)
            part = score[row * half : (row + 1) * half, col * half : (col + 1) * half]
            mixed = (part * decay).astype(jnp.bfloat16)
            term = contract(mixed, scaled[col * half : (col + 1) * half], 1, 0)
            sums[row] = term if sums[row] is None else sums[row] + term
    for row in range(2):
        rows = slice(row * half, (row + 1) * half)
        y_ref[rows, :] = sums[row] + skip_ref[...] * x[rows]


def scan_bwd_kernel(
    x_ref, dt_ref, cum_ref, cumt_ref, b_ref, c_ref, skip_ref, dy_ref,
    dx_ref, ddt_ref, drow_ref, dcol_ref, db_ref, dc_ref, dskip_ref, score, dscore,
):
    pair = pl.program_id(0)
    length = x_ref.shape[0]
    half, tiles = tiles_of(length)

    @pl.when(pair == 0)
    def _():
        score[...] = contract(c_ref[...], b_ref[...], 1, 1, HIGH)
        dscore[...] = jnp.zeros_like(dscore)
        ddt_ref[...] = jnp.zeros_like(ddt_ref)
        drow_ref[...] = jnp.zeros_like(drow_ref)

    which = pair_lanes(x_ref.shape)
    lane = lax.broadcasted_iota(jnp.int32, x_ref.shape, 1)
    x = x_ref[...]
    dy = dy_ref[...]
    dskip_ref[...] = jnp.sum(x * dy, axis=0, keepdims=True)
    d_scaled = [None, None]
    dt_pair = jnp.zeros_like(x)
    for sub in range(PAIR):
        head = pair * PAIR + sub
        cum_col = column_of(cum_ref[...], head)
        cum_row = cumt_ref[pl.ds(head, 1), :]
        dt_here = jnp.where(which == sub, column_of(dt_ref[...], head), 0.0)
        dt_pair = dt_pair + dt_here
        scaled = (x * dt_here).astype(jnp.bfloat16)
        dy_here = jnp.where(which == sub, dy, 0.0).astype(jnp.bfloat16)
        row_sum = [None, None]
        col_sum = [None, None]
        for row, col in tiles:
            rows = slice(row * half, (row + 1) * half)
            cols = slice(col * half, (col + 1) * half)
            decay = decay_tile(cum_col, cum_row, half, row, col)
            part = score[rows, cols]
            mixed = (part * decay).astype(jnp.bfloat16)
            d_mixed = contract(dy_here[rows], scaled[cols], 1, 1) * decay
            dscore[rows, cols] += d_mixed
            weight = d_mixed * part
            over_cols = jnp.sum(weight, axis=1, keepdims=True)
            over_rows = jnp.sum(weight, axis=0, keepdims=True)
            term = contract(mixed, dy_here[rows], 0, 0)
            row_sum[row] = over_cols if row_sum[row] is None else row_sum[row] + over_cols
            col_sum[col] = over_rows if col_sum[col] is None else col_sum[col] + over_rows
            d_scaled[col] = term if d_scaled[col] is None else d_scaled[col] + term
        for part_index in range(2):
            span = slice(part_index * half, (part_index + 1) * half)
            drow_ref[span, :] = jnp.where(lane[span] == head, row_sum[part_index], drow_ref[span, :])
            dcol_ref[pl.ds(head, 1), span] = col_sum[part_index]
    for part_index in range(2):
        span = slice(part_index * half, (part_index + 1) * half)
        dx_ref[span, :] = d_scaled[part_index] * dt_pair[span] + skip_ref[...] * dy[span]
        products = d_scaled[part_index] * x[span]
        for sub in range(PAIR):
            head = pair * PAIR + sub
            total = jnp.sum(
                jnp.where(which[span] == sub, products, 0.0), axis=1, keepdims=True
            )
            ddt_ref[span, :] = jnp.where(lane[span] == head, total, ddt_ref[span, :])

    @pl.when(pair == pl.num_programs(0) - 1)
    def _():
        dc_ref[...] = contract(dscore[...], b_ref[...], 1, 0, HIGH)
        db_ref[...] = contract(dscore[...], c_ref[...], 0, 0, HIGH)


def whole_spec(shape):
    return pl.BlockSpec(shape, lambda pair: (0, 0))


def scan_operands(active, dt, cum, skip):
    pad = ((0, 0), (0, LANES - NH))
    return active, jnp.pad(dt, pad), jnp.pad(cum, pad), cum.T, active, active, skip


def scan_specs(length):
    lanes = whole_spec((length, LANES))
    return [
        pl.BlockSpec((length, LANES), lambda pair: (0, pair)),
        lanes,
        lanes,
        whole_spec((NH, length)),
        pl.BlockSpec((length, NS), lambda pair: (0, DI // NS)),
        pl.BlockSpec((length, NS), lambda pair: (0, DI // NS + 1)),
        pl.BlockSpec((1, LANES), lambda pair: (0, pair)),
    ]


@jax.custom_vjp
def span_scan(active, dt, cum, skip):
    length = active.shape[0]
    return pl.pallas_call(
        scan_fwd_kernel,
        grid=(NH // PAIR,),
        in_specs=scan_specs(length),
        out_specs=pl.BlockSpec((length, LANES), lambda pair: (0, pair)),
        out_shape=jax.ShapeDtypeStruct((length, DI), jnp.float32),
        scratch_shapes=[pltpu.VMEM((length, length), jnp.float32)],
        name="scan_fwd",
    )(*scan_operands(active, dt, cum, skip))


def span_scan_fwd(active, dt, cum, skip):
    return span_scan(active, dt, cum, skip), (active, dt, cum, skip)


def span_scan_bwd(saved, dy):
    active, dt, cum, skip = saved
    length = active.shape[0]
    pair_block = pl.BlockSpec((length, LANES), lambda pair: (0, pair))
    lanes = whole_spec((length, LANES))
    square = pltpu.VMEM((length, length), jnp.float32)
    f32 = jnp.float32
    dx, ddt, drow, dcol, db, dc, dskip = pl.pallas_call(
        scan_bwd_kernel,
        grid=(NH // PAIR,),
        in_specs=scan_specs(length) + [pair_block],
        out_specs=[
            pair_block, lanes, lanes, whole_spec((NH, length)),
            whole_spec((length, NS)), whole_spec((length, NS)),
            pl.BlockSpec((1, LANES), lambda pair: (0, pair)),
        ],
        out_shape=[
            jax.ShapeDtypeStruct((length, DI), f32),
            jax.ShapeDtypeStruct((length, LANES), f32),
            jax.ShapeDtypeStruct((length, LANES), f32),
            jax.ShapeDtypeStruct((NH, length), f32),
            jax.ShapeDtypeStruct((length, NS), f32),
            jax.ShapeDtypeStruct((length, NS), f32),
            jax.ShapeDtypeStruct((1, DI), f32),
        ],
        scratch_shapes=[square, square],
        name="scan_bwd",
    )(*scan_operands(active, dt, cum, skip), dy)
    d_active = jnp.concatenate([dx, db, dc], axis=1)
    return d_active, ddt[:, :NH], drow[:, :NH] - dcol.T, dskip


span_scan.defvjp(span_scan_fwd, span_scan_bwd)


def mixer_core(proj, conv_w, conv_b, step_bias, decay_log, skip_weight, mix_gain):
    length = proj.shape[0]
    gate = proj[:, :DI]
    conv_in = proj[:, DI : DI + CONV_CH]
    step_raw = proj[:, DI + CONV_CH :]
    padded = jnp.pad(conv_in, ((KCONV - 1, 0), (0, 0)))
    conv_out = jnp.zeros_like(conv_in) + conv_b
    for offset in range(KCONV):
        conv_out = conv_out + conv_w[offset] * padded[offset : offset + length]
    active = jax.nn.silu(conv_out)
    step = jax.nn.softplus(step_raw + step_bias)
    logdecay = -step * jnp.exp(decay_log)
    causal = (jnp.arange(length)[:, None] >= jnp.arange(length)[None, :]).astype(jnp.float32)
    cum = jnp.dot(causal, logdecay, precision=HIGH)
    mixed = span_scan(active, step, cum, jnp.repeat(skip_weight, HD)[None])
    flat = mixed * jax.nn.silu(gate)
    scale = lax.rsqrt(jnp.mean(flat * flat, axis=-1, keepdims=True) + EPS)
    return flat * scale * mix_gain


def bits_of(axis):
    size = lax.axis_size(axis)
    return [(axis, 1 << k) for k in reversed(range(size.bit_length() - 1))]


def all_labels():
    return bits_of("fsdp") + bits_of("rep")


def my_bit(label):
    return (lax.axis_index(label[0]) // label[1]) % 2


def partner(label):
    ids = {name: lax.axis_index(name) for name in ("fsdp", "rep")}
    ids[label[0]] = ids[label[0]] + label[1] * (1 - 2 * my_bit(label))
    return (ids["fsdp"], ids["rep"])


def greet(labels):
    barrier = pltpu.get_barrier_semaphore()
    for label in labels:
        pl.semaphore_signal(
            barrier, inc=1, device_id=partner(label), device_id_type=pl.DeviceIdType.MESH
        )
    pl.semaphore_wait(barrier, len(labels))


def send(source, target, sems, stream, slot, label):
    copy = pltpu.make_async_remote_copy(
        src_ref=source,
        dst_ref=target,
        send_sem=sems[0].at[stream, slot],
        recv_sem=sems[1].at[stream, slot],
        device_id=partner(label),
        device_id_type=pl.DeviceIdType.MESH,
    )
    copy.start()
    return copy


def orders():
    fsdp, rep = bits_of("fsdp"), bits_of("rep")
    near, wide = fsdp[-1:], fsdp[:-1]
    mid, far = wide[-1:], wide[:-1]
    core, row = rep[-1:], rep[:-1]
    return (
        core + row + near + mid + far,
        core + near + mid + row + far,
        core + mid + row + near + far,
    )


def position(order):
    place = 0
    for label in order:
        place = place * 2 + my_bit(label)
    return place


def gather_kernel(plan, *refs):
    count = len(plan)
    ins, outs = refs[:count], refs[count : 2 * count]
    sems, local = refs[2 * count : 2 * count + 2], refs[2 * count + 2]
    greet(all_labels())
    steps = max(len(order) for order in plan)
    open_sends, waiting, locals_ = [], {}, []
    for k in range(count):
        copy = pltpu.make_async_copy(ins[k], outs[k].at[pl.ds(position(plan[k]), 1)], local.at[k])
        copy.start()
        locals_.append(copy)
    for step in range(steps):
        for k, order in enumerate(plan):
            if step >= len(order):
                continue
            size = 1 << step
            start = position(order) // size * size
            if step == 0:
                source = ins[k]
            else:
                if step == 1:
                    locals_[k].wait()
                waiting[k].wait_recv()
                source = outs[k].at[pl.ds(start, size)]
            label = order[len(order) - 1 - step]
            copy = send(source, outs[k].at[pl.ds(start, size)], sems, k, step, label)
            waiting[k] = copy
            open_sends.append(copy)
    for k in range(count):
        waiting[k].wait_recv()
        if len(plan[k]) < 2:
            locals_[k].wait()
    for copy in open_sends:
        copy.wait_send()


def gather_all(plan, pieces):
    steps = max(len(order) for order in plan)
    vmem = pl.BlockSpec(memory_space=pltpu.VMEM)
    return pl.pallas_call(
        functools.partial(gather_kernel, plan),
        in_specs=[vmem] * len(pieces),
        out_specs=[vmem] * len(pieces),
        out_shape=[
            jax.ShapeDtypeStruct((1 << len(order),) + piece.shape[1:], piece.dtype)
            for order, piece in zip(plan, pieces)
        ],
        scratch_shapes=[
            pltpu.SemaphoreType.DMA((len(pieces), steps)),
            pltpu.SemaphoreType.DMA((len(pieces), steps)),
            pltpu.SemaphoreType.DMA((len(pieces),)),
        ],
        compiler_params=pltpu.CompilerParams(
            collective_id=0, has_side_effects=True, vmem_limit_bytes=60 << 20
        ),
        name="gather_weights",
    )(*pieces)


def reduce_kernel(plan, tail, *refs):
    count = len(plan)
    steps = len(plan[0])
    grads, vector = refs[:count], refs[count]
    outs, total = refs[count + 1 : 2 * count + 1], refs[2 * count + 1]
    at = 2 * count + 2
    held = [refs[at + k * steps : at + (k + 1) * steps] for k in range(count)]
    at += count * steps
    sums = refs[at : at + steps]
    sems, local = refs[at + steps : at + steps + 2], refs[at + steps + 2]
    labels = all_labels()
    greet(labels)
    open_sends, waiting = [], {}
    vector_order = labels[::-1]

    def source_of(k, step):
        return grads[k] if step == 0 else held[k][step - 1]

    def add_in(k, step):
        size = 1 << (steps - 1 - step)
        base = source_of(k, step)
        target = held[k][step]
        start = my_bit(plan[k][step]) * size

        def one(i, carry):
            left = base[start + i].astype(jnp.float32)
            target[i] = (left + target[i].astype(jnp.float32)).astype(target.dtype)
            return carry

        lax.fori_loop(0, size, one, 0)

    for step in range(steps):
        for k in range(count):
            if step > 0:
                waiting[k].wait_recv()
                add_in(k, step - 1)
            label = plan[k][step]
            size = 1 << (steps - 1 - step)
            away = source_of(k, step).at[pl.ds((1 - my_bit(label)) * size, size)]
            waiting[k] = send(away, held[k][step], sems, k, step, label)
            open_sends.append(waiting[k])
        if step > 0:
            waiting[count].wait_recv()
            before = vector if step == 1 else sums[step - 2]
            sums[step - 1][...] = before[...] + sums[step - 1][...]
        now = vector if step == 0 else sums[step - 1]
        waiting[count] = send(now, sums[step], sems, count, step, vector_order[step])
        open_sends.append(waiting[count])

    here = lax.axis_index("rep")
    known = {k: [0] for k in range(count)}
    inbox = {k: [] for k in range(count)}
    for hop, label in enumerate(tail):
        for k in range(count):
            if hop == 0:
                waiting[k].wait_recv()
                add_in(k, steps - 1)
                copy = pltpu.make_async_copy(
                    held[k][steps - 1], outs[k].at[pl.ds(here, 1)], local.at[k]
                )
                copy.start()
                waiting[k] = copy
            for copy in inbox[k]:
                copy.wait_recv()
            inbox[k] = []
            shift = label[1] * (1 - 2 * my_bit(label))
            for n, offset in enumerate(list(known[k])):
                place = pl.ds(here + offset, 1)
                source = held[k][steps - 1] if n == 0 else outs[k].at[place]
                copy = send(source, outs[k].at[place], sems, k, steps + (1 << hop) - 1 + n, label)
                inbox[k].append(copy)
                open_sends.append(copy)
                known[k].append(offset + shift)
    waiting[count].wait_recv()
    before = sums[steps - 2]
    total[...] = before[...] + sums[steps - 1][...]
    for k in range(count):
        for copy in inbox[k]:
            copy.wait_recv()
        waiting[k].wait()
    for copy in open_sends:
        copy.wait_send()


def reduce_all(plan, grads, vector):
    steps = len(plan[0])
    reps = lax.axis_size("rep")
    vmem = pl.BlockSpec(memory_space=pltpu.VMEM)
    slots = pltpu.SemaphoreType.DMA((len(grads) + 1, steps + reps))
    scratch = []
    for grad in grads:
        scratch += [
            pltpu.VMEM((1 << (steps - 1 - step),) + grad.shape[1:], grad.dtype)
            for step in range(steps)
        ]
    scratch += [pltpu.VMEM(vector.shape, vector.dtype) for _ in range(steps)]
    return pl.pallas_call(
        functools.partial(reduce_kernel, plan, bits_of("rep")),
        in_specs=[vmem] * (len(grads) + 1),
        out_specs=[vmem] * (len(grads) + 1),
        out_shape=[jax.ShapeDtypeStruct((reps,) + g.shape[1:], g.dtype) for g in grads]
        + [jax.ShapeDtypeStruct(vector.shape, vector.dtype)],
        scratch_shapes=scratch + [slots, slots, pltpu.SemaphoreType.DMA((len(grads),))],
        compiler_params=pltpu.CompilerParams(
            collective_id=1, has_side_effects=True, vmem_limit_bytes=60 << 20
        ),
        name="reduce_grads",
    )(*grads, vector)


def to_order(array, order):
    labels = all_labels()
    rows = array.shape[0] >> len(labels)
    perm = [labels.index(label) for label in order] + [len(labels), len(labels) + 1]
    split = array.reshape((2,) * len(labels) + (rows, array.shape[1]))
    return split.transpose(perm).reshape((-1, rows, array.shape[1]))


def from_order(blocks, order):
    labels = all_labels()
    perm = [order.index(label) for label in labels] + [len(labels), len(labels) + 1]
    split = blocks.reshape((2,) * len(labels) + blocks.shape[1:])
    return split.transpose(perm).reshape((-1, blocks.shape[-1]))


def whole_lanes(array):
    return jnp.pad(array, ((0, 0), (0, -array.shape[1] % LANES)))


def my_rows(shard):
    count = shard.shape[0] // lax.axis_size("rep")
    return lax.dynamic_slice_in_dim(shard, lax.axis_index("rep") * count, count, 0)


def body(
    hidden_in, cotangent, lengths, norm_gain, in_weight, conv_weight, conv_bias,
    step_bias, decay_log, skip_weight, mix_gain, out_weight,
):
    plan = orders()
    columns = [slice(CUTS[k], CUTS[k + 1]) for k in range(len(CUTS) - 1)]
    width = out_weight.shape[1] // len(columns)
    out_columns = [slice(k * width, (k + 1) * width) for k in range(len(columns))]
    small = jnp.concatenate([norm_gain, conv_weight.reshape(-1), conv_bias, mix_gain])
    small = jnp.pad(small, (0, -small.size % 2048)).reshape(1, -1, LANES)
    in_rows, out_rows = my_rows(in_weight), my_rows(out_weight)
    pieces = [small] + [in_rows[None, :, cut] for cut in columns]
    pieces += [out_rows[None, :, cut] for cut in out_columns]
    wide_plan = list(plan) + list(plan)
    gathered = gather_all([bits_of("fsdp")] + wide_plan, pieces)
    full = [from_order(blocks, order) for blocks, order in zip(gathered[1:], wide_plan)]
    in_full = jnp.concatenate(full[: len(columns)], axis=1)
    out_full = jnp.concatenate(full[len(columns) :], axis=1)
    small = gathered[0].reshape(lax.axis_size("fsdp"), -1)
    groups = small.shape[0]
    ends = [norm_gain.size, conv_weight.size, conv_bias.size]
    cut_a, cut_b, cut_c = ends[0], ends[0] + ends[1], sum(ends)
    gain_full = small[:, :cut_a].reshape(-1)
    conv_full = small[:, cut_a:cut_b].reshape(groups, KCONV, -1).transpose(1, 0, 2)
    conv_full = conv_full.reshape(KCONV, -1)
    bias_full = small[:, cut_b:cut_c].reshape(-1)
    mix_full = small[:, cut_c : cut_c + mix_gain.size].reshape(-1)

    seq_count = lengths.shape[0]
    rows_here = hidden_in.shape[0]
    length = rows_here // seq_count

    def core(proj, *params):
        parts = [
            mixer_core(proj[s * length : (s + 1) * length], *params) for s in range(seq_count)
        ]
        return parts[0] if seq_count == 1 else jnp.concatenate(parts)

    resid = hidden_in.astype(jnp.float32)
    normed, norm_back = jax.vjp(pre_norm, resid, gain_full.astype(jnp.float32))
    normed_b = normed.astype(jnp.bfloat16)
    proj = jnp.dot(normed_b, in_full, preferred_element_type=jnp.float32)
    gated, core_back = jax.vjp(
        core,
        proj,
        conv_full.astype(jnp.float32),
        bias_full.astype(jnp.float32),
        step_bias,
        decay_log,
        skip_weight,
        mix_full.astype(jnp.float32),
    )
    gated_b = gated.astype(jnp.bfloat16)
    branch = jnp.dot(gated_b, out_full, preferred_element_type=jnp.float32)
    live = (
        (jnp.arange(length)[None, :] < lengths[:, None]).reshape(rows_here, 1).astype(jnp.float32)
    )
    block_out = (resid + live * branch).astype(jnp.bfloat16)
    cot_live = cotangent * live.astype(jnp.bfloat16)
    d_out_w = contract(gated_b, cot_live, 0, 0)
    d_gated = contract(cot_live, out_full, 1, 1)
    d_proj, d_cw, d_cb, d_sb, d_dl, d_sk, d_mg = core_back(d_gated)
    d_proj_b = d_proj.astype(jnp.bfloat16)
    d_normed = contract(d_proj_b, in_full, 1, 1)
    d_resid, d_gain = norm_back(d_normed)
    grad_in = cotangent.astype(jnp.float32) + d_resid

    vectors = [d_gain, d_cw.reshape(-1), d_cb, d_mg, d_sb, d_dl, d_sk]
    packed = jnp.concatenate(vectors)
    packed = jnp.pad(packed, (0, -packed.size % 1024)).reshape(-1, LANES)
    partial = [contract(normed_b, whole_lanes(d_proj_b[:, cut]), 0, 0) for cut in columns]
    partial += [d_out_w[:, cut] for cut in out_columns]
    blocks = [
        to_order(part.astype(jnp.bfloat16), order) for part, order in zip(partial, wide_plan)
    ]
    *sums, packed = reduce_all(wide_plan, blocks, packed)
    sums = [part.reshape(-1, part.shape[-1]) for part in sums]
    g_in = jnp.concatenate(sums[: len(columns)], axis=1)[:, :PROJ].astype(jnp.float32)
    g_out = jnp.concatenate(sums[len(columns) :], axis=1).astype(jnp.float32)
    packed = packed.reshape(-1)
    totals = []
    at = 0
    for vector in vectors:
        totals.append(packed[at : at + vector.size])
        at += vector.size
    me = lax.axis_index("fsdp")

    def mine(array, dim):
        count = array.shape[dim] // groups
        return lax.dynamic_slice_in_dim(array, me * count, count, dim)

    g_gain = mine(totals[0], 0)
    g_cw = mine(totals[1].reshape(KCONV, -1), 1)
    g_cb = mine(totals[2], 0)
    g_mg = mine(totals[3], 0)
    g_sb, g_dl, g_sk = totals[4:]
    return (block_out, grad_in, g_gain, g_in, g_cw, g_cb, g_sb, g_dl, g_sk, g_mg, g_out)


def solution(mesh):
    in_specs = (
        P(("fsdp", "rep"), None),
        P(("fsdp", "rep"), None),
        P(("fsdp", "rep")),
        P("fsdp"),
        P("fsdp", None),
        P(None, "fsdp"),
        P("fsdp"),
        P(),
        P(),
        P(),
        P("fsdp"),
        P("fsdp", None),
    )
    out_specs = (
        P(("fsdp", "rep"), None),
        P(("fsdp", "rep"), None),
        P("fsdp"),
        P("fsdp", None),
        P(None, "fsdp"),
        P("fsdp"),
        P(),
        P(),
        P(),
        P("fsdp"),
        P("fsdp", None),
    )
    return jax.shard_map(body, mesh=mesh, in_specs=in_specs, out_specs=out_specs, check_vma=False)
```

profile of v0, /device:TPU:0, one launch (start us, length us, event | category | flops | bytes accessed | tf_op | source)
XLA Modules:
  0.0 252.2 jit_solution(6823790517469977771)
XLA Ops:
  5.2 2.1 concatenate.21
  9.8 1.4 dynamic-slice_bitcast_fusion.refs_3_
  11.3 1.4 dynamic-slice_bitcast_fusion.3
  12.7 1.5 dynamic-slice_bitcast_fusion.1
  14.2 50.0 %gather_weights.1 = (bf16[8,16,128]{2,1,0:T(8,128)(2,1)}, bf16[32,24,1152]{2,1,0:T(8,128)(2,1)}, bf16[32,24,1152]{2,1,0:T(8,128)(2,1)}, bf16[32,24,1048]{2,1,0:T...) custom-call(bf16[1,16,128]{2,1,0:T(8,128)(2,1)} %pad_bitcast_fusion.1.refs_0_, ...), custom_call_target="tpu_custom_call" | custom-call | tf_op jit(solution)/shard_map/gather_weights/pallas_call | solution.py:355
  65.1 1.7 copy.55
  69.7 2.1 copy.62
  73.7 1.7 copy.56
  75.7 3.1 %fusion.7 = f32[512,3352]{1,0:T(8,128)S(1)} fusion(bf16[768,1048]{1,0:T(8,128)(2,1)S(1)} %bitcast.106, bf16[768,1152]{1,0:T(8,128)(2,1)S(1)} %bitcast.104, bf16[768,1152]{1,0:T(8,128)(2,1)S(1)} %bitcast.102, bf16[512,768]{1,0:T(8,128)(2,1)S(1)} %copy-done.7, f32[768]{0:T(1024)S(1)} %reshape.314, f32[512]{0:T(512)S(1)} %fusion.39), kind=kOutput, calls=%fused_computation.39 | convolution fusion | flops 2653138944 | bytes 12805120 | tf_op jit(solution)/shard_map/dot_general | solution.py:550
  78.8 2.9 %copy-done.3 = f32[512,3352]{1,0:T(8,128)} copy-done((f32[512,3352]{1,0:T(8,128)}, f32[512,3352]{1,0:T(8,128)S(1)}, u32[]{:S(2)}) %copy-start.3) | copy-done | bytes 6864920
  84.0 2.3 slice.170
  86.3 1.9 copy-done
  88.2 4.2 %fusion.2 = (f32[512,1792]{1,0:T(8,128)}, f32[512,1792]{1,0:T(8,128)}) fusion(f32[512,1792]{1,0:T(8,128)S(1)} %slice.170, f32[1792]{0:T(1024)S(1)} %mul.304, f32[1792]{0:T(1024)S(1)} %mul.301, f32[1792]{0:T(1024)S(1)} %copy-done.28, f32[1792]{0:T(1024)S(1)} %mul.290, f32[1792]{0:T(1024)S(1)} %copy-done.31), kind=kLoop, calls=%fused_computation.15 | loop fusion | flops 11010048 | bytes 11045888 | tf_op jit(solution)/shard_map/jvp(jit(silu))/mul | solution.py:245
  92.4 12.7 %jvp_scan_fwd_.1 = f32[512,1536]{1,0:T(8,128)} custom-call(f32[512,1792]{1,0:T(8,128)} %get-tuple-element.71.x_ref.b_ref.c_ref, f32[512,128]{1,0:T(8,128)} %pad.65.dt_ref, f32[512,128]{1,0:T(8,128)} %pad.66.cum_ref, f32[24,512]{1,0:T(8,128)} %bitcast.123, f32[512,1792]{1,0:T(8,128)} %get-tuple-element.71.x_ref.b_ref.c_ref, ...), custom_call_target="tpu_custom_call" | custom-call | tf_op jit(solution)/shard_map/jvp(scan_fwd)/pallas_call | solution.py:186
  105.2 4.0 %multiply_reduce_fusion.6 = (f32[512]{0:T(512)S(1)}, f32[512,1536]{1,0:T(8,128)S(1)}) fusion(f32[512,1536]{1,0:T(8,128)} %jvp_scan_fwd_.1, f32[512,3352]{1,0:T(8,128)} %copy-done.3), kind=kLoop, calls=%fused_computation.28 | loop fusion | flops 5504512 | bytes 9439232 | tf_op jit(solution)/shard_map/jvp()/reduce_sum | solution.py:252
  109.2 2.3 fusion.14
  111.6 2.3 multiply_reduce_fusion.4
  113.9 5.5 %fusion.16 = (f32[512,1536]{1,0:T(8,128)}, f32[512,1536]{1,0:T(8,128)}) fusion(f32[512,1536]{1,0:T(8,128)S(1)} %get-tuple-element.70, f32[512]{0:T(512)S(1)} %multiply_multiply_fusion.1, f32[512,1536]{1,0:T(8,128)S(1)} %get-tuple-element.91, f32[1536]{0:T(1024)S(1)} %copy-done.30, f32[512]{0:T(512)S(1)} %fusion.40, f32[512,3352]{1,0:T(8,128)} %copy-done.3, ...), kind=kLoop, calls=%fused_computation.52 | loop fusion | flops 13369344 | bytes 18884608 | tf_op jit(solution)/shard_map/transpose(jvp())/mul | solution.py:251
  119.4 3.0 %convolution_convert_fusion = bf16[1536,768]{1,0:T(8,128)(2,1)} fusion(bf16[512,768]{1,0:T(8,128)(2,1)S(1)} %copy-done.16, bf16[512]{0:T(512)(128)(2,1)S(1)} %copy-done.42, f32[512,1536]{1,0:T(8,128)S(1)} %get-tuple-element.70, f32[1536]{0:T(1024)S(1)} %copy-done.30, f32[512]{0:T(512)S(1)} %fusion.40), kind=kOutput, calls=%fused_computation.19 | convolution fusion | flops 1211891712 | bytes 6300672 | tf_op jit(solution)/shard_map/dot_general | solution.py:32
  122.4 22.3 %transpose_jvp_scan_bwd__.1 = (f32[512,1536]{1,0:T(8,128)}, f32[512,128]{1,0:T(8,128)}, f32[512,128]{1,0:T(8,128)}, f32[24,512]{1,0:T(8,128)}, f32[512,128]{1,0:...) custom-call(f32[512,1792]{1,0:T(8,128)} %get-tuple-element.71.x_ref.b_ref.c_ref, f32[512,128]{1,0:T(8,128)} %pad.65.dt_ref, ...), custom_call_target="tpu_custom_call" | custom-call | tf_op jit(solution)/shard_map/transpose(jvp(scan_bwd))/pallas_call | solution.py:250
  144.7 1.8 fusion.55
  150.4 3.0 %fusion.51 = (f32[24]{0:T(128)}, f32[512,24]{1,0:T(8,128)}, f32[24]{0:T(128)S(1)}) fusion(f32[512,24]{1,0:T(8,128)S(1)} %compare_select_fusion.2, f32[24]{0:T(128)S(1)} %copy-done.43, f32[512,3352]{1,0:T(8,128)} %copy-done.3, f32[24]{0:T(128)S(1)} %copy-done.48, f32[512,128]{1,0:T(8,128)} %get-tuple-element.39, f32[512,128]{0,1:T(8,128)S(1)} %copy.65, ...), kind=kOutput, calls=%fused_computation.123 | convolution fusion | flops 76206032 | bytes 509120 | tf_op jit(solution)/shard_map/transpose(jvp())/dot_general | solution.py:249
  155.2 1.7 copy-done.4
  158.1 6.5 %multiply_reduce_fusion.2 = (f32[1792]{0:T(1024)S(1)}, f32[1792]{0:T(1024)S(1)}, f32[1792]{0:T(1024)S(1)}, f32[1792]{0:T(1024)}, f32[1792]{0:T(1024)S(1)}, /*index=5*/f32[512,1792]{1,0:T(8,128)}) fusion(f32[512,1792]{1,0:T(8,128)S(1)} %copy-done.1, f32[512,3352]{1,0:T(8,128)} %copy-done.3, f32[512,1792]{1,0:T(8,128)S(1)} %copy-done.4, ...), kind=kLoop, calls=%fused_computation.12 | loop fusion | flops 16506112 | bytes 18385920 | tf_op jit(solution)/shard_map/transpose(jvp())/reduce_sum | solution.py:244
  165.3 3.2 %broadcast_multiply_fusion = (f32[512,1792]{1,0:T(8,128)S(1)}, f32[512,1792]{1,0:T(8,128)S(1)}, f32[512,1792]{1,0:T(8,128)S(1)}, f32[512,1792]{1,0:T(8,128)S(1)}) fusion(f32[512,1792]{1,0:T(8,128)} %get-tuple-element.68, f32[1792]{0:T(1024)S(1)} %mul.304, f32[1792]{0:T(1024)S(1)} %mul.290, f32[1792]{0:T(1024)S(1)} %copy-done.28, f32[1792]{0:T(1024)S(1)} %mul.301), kind=kLoop, calls=%fused_computation.42 | loop fusion | flops 3670016 | bytes 18378752 | tf_op jit(solution)/shard_map/transpose(jvp())/mul | solution.py:244
  169.7 2.5 add_convert_fusion
  173.2 3.3 %fusion.11 = (f32[768]{0:T(1024)S(1)}, f32[512]{0:T(512)S(1)}, f32[512,768]{1,0:T(8,128)S(1)}) fusion(bf16[512,768]{1,0:T(8,128)(2,1)S(1)} %copy-done.7, f32[512]{0:T(512)S(1)} %copy-done.37, f32[768]{0:T(1024)S(1)} %copy-done.35, bf16[512,3352]{1,0:T(8,128)(2,1)S(1)} %add_convert_fusion, bf16[768,1048]{1,0:T(8,128)(2,1)S(1)} %bitcast.107, ...), kind=kOutput, calls=%fused_computation.47 | convolution fusion | flops 2654317312 | bytes 10950656 | tf_op jit(solution)/shard_map/dot_general | solution.py:32
  177.3 1.6 fusion.12
  187.0 54.3 %reduce_grads.1 = (bf16[4,24,1152]{2,1,0:T(8,128)(2,1)}, bf16[4,24,1152]{2,1,0:T(8,128)(2,1)}, bf16[4,24,1152]{2,1,0:T(8,128)(2,1)}, bf16[4,48,256]{2,1,0:T(8,12...) custom-call(bf16[32,24,1152]{2,1,0:T(8,128)(2,1)} %bitcast.94, ...), custom_call_target="tpu_custom_call" | custom-call | tf_op jit(solution)/shard_map/reduce_grads/pallas_call | solution.py:471
  241.3 1.4 fusion.56
  248.1 1.8 maximum_convert_fusion
  249.9 2.3 fusion.25
  (165 shorter events, 38.2 us)
Async XLA Ops:
  4.4 71.2 %copy-start.36 = (f32[512]{0:T(512)}, f32[512]{0:T(512)S(1)}, u32[]{:S(2)}) copy-start(f32[512]{0:T(512)S(1)} %fusion.39) | copy-start | bytes 6148
  64.2 7.6 %copy-start.19 = (bf16[32,48,256]{2,1,0:T(8,128)(2,1)S(1)}, bf16[32,48,256]{2,1,0:T(8,128)(2,1)}, u32[]{:S(2)}) copy-start(bf16[32,48,256]{2,1,0:T(8,128)(2,1)} %get-tuple-element.37) | copy-start | bytes 2359300
  65.0 7.7 %copy-start.18 = (bf16[32,48,256]{2,1,0:T(8,128)(2,1)S(1)}, bf16[32,48,256]{2,1,0:T(8,128)(2,1)}, u32[]{:S(2)}) copy-start(bf16[32,48,256]{2,1,0:T(8,128)(2,1)} %get-tuple-element.38) | copy-start | bytes 2359300
  66.7 8.9 %copy-start.9 = (bf16[2,2,2,2,2,24,1152]{6,5,0,1,2,3,4:T(8,128)(2,1)}, bf16[2,2,2,2,2,24,1152]{6,5,0,1,2,3,4:T(8,128)(2,1)S(1)}, u32[]{:S(2)}) copy-start(bf16[2,2,2,2,2,24,1152]{6,5,0,1,2,3,4:T(8,128)(2,1)S(1)} %copy.55) | copy-start | bytes 5308420
  66.8 8.8 %copy-start.34 = (f32[768]{0:T(1024)}, f32[768]{0:T(1024)S(1)}, u32[]{:S(2)}) copy-start(f32[768]{0:T(1024)S(1)} %reshape.314) | copy-start | bytes 9220
  71.8 3.6 %copy-start.15 = (bf16[32,24,1048]{2,1,0:T(8,128)(2,1)S(1)}, bf16[32,24,1048]{2,1,0:T(8,128)(2,1)}, u32[]{:S(2)}) copy-start(bf16[32,24,1048]{2,1,0:T(8,128)(2,1)} %get-tuple-element.35) | copy-start | bytes 4829188
  75.6 6.1 %copy-start.43 = (f32[24]{0:T(128)S(1)}, f32[24]{0:T(128)}, u32[]{:S(2)}) copy-start(f32[24]{0:T(128)} %param.19) | copy-start | bytes 292
  75.6 6.2 %copy-start.48 = (f32[24]{0:T(128)S(1)}, f32[24]{0:T(128)}, u32[]{:S(2)}) copy-start(f32[24]{0:T(128)} %exp.21) | copy-start | bytes 292
  82.4 3.9 %copy-start.23 = (f32[512,24]{0,1:T(8,128)}, f32[512,24]{0,1:T(8,128)S(1)}, u32[]{:S(2)}) copy-start(f32[512,24]{0,1:T(8,128)S(1)} %fusion.21) | copy-start | bytes 147460
  84.0 4.2 %copy-start.28 = (f32[1792]{0:T(1024)S(1)}, f32[1792]{0:T(1024)}, u32[]{:S(2)}) copy-start(f32[1792]{0:T(1024)} %mul.298) | copy-start | bytes 21508
  84.0 4.2 %copy-start.31 = (f32[1792]{0:T(1024)S(1)}, f32[1792]{0:T(1024)}, u32[]{:S(2)}) copy-start(f32[1792]{0:T(1024)} %reshape.313) | copy-start | bytes 21508
  105.1 4.0 %copy-start.20 = (bf16[2,2,2,2,2,48,256]{6,5,0,1,2,3,4:T(8,128)(2,1)S(1)}, bf16[2,2,2,2,2,48,256]{6,5,0,1,2,3,4:T(8,128)(2,1)}, u32[]{:S(2)}) copy-start(bf16[2,2,2,2,2,48,256]{6,5,0,1,2,3,4:T(8,128)(2,1)} %copy.62) | copy-start | bytes 2359300
  105.1 4.0 %copy-start.21 = (bf16[2,2,2,2,2,48,256]{6,5,0,3,1,2,4:T(8,128)(2,1)S(1)}, bf16[2,2,2,2,2,48,256]{6,5,0,3,1,2,4:T(8,128)(2,1)}, u32[]{:S(2)}) copy-start(bf16[2,2,2,2,2,48,256]{6,5,0,3,1,2,4:T(8,128)(2,1)} %copy.63) | copy-start | bytes 2359300
  105.1 4.0 %copy-start.22 = (bf16[2,2,2,2,2,48,256]{6,5,0,2,3,1,4:T(8,128)(2,1)S(1)}, bf16[2,2,2,2,2,48,256]{6,5,0,2,3,1,4:T(8,128)(2,1)}, u32[]{:S(2)}) copy-start(bf16[2,2,2,2,2,48,256]{6,5,0,2,3,1,4:T(8,128)(2,1)} %copy.64) | copy-start | bytes 2359300
  105.1 4.0 %copy-start.30 = (f32[1536]{0:T(1024)S(1)}, f32[1536]{0:T(1024)}, u32[]{:S(2)}) copy-start(f32[1536]{0:T(1024)} %reshape.315) | copy-start | bytes 18436
  105.2 4.0 %copy-start.41 = (f32[512]{0:T(512)S(1)}, f32[512]{0:T(512)}, u32[]{:S(2)}) copy-start(f32[512]{0:T(512)} %get-tuple-element.93) | copy-start | bytes 6148
  144.7 3.8 %copy-start.39 = (f32[1,1536]{1,0:T(1,128)S(1)}, f32[1,1536]{1,0:T(1,128)}, u32[]{:S(2)}) copy-start(f32[1,1536]{1,0:T(1,128)} %get-tuple-element.45) | copy-start | bytes 18436
  144.7 5.7 %copy-start.46 = (f32[24,512]{1,0:T(8,128)S(1)}, f32[24,512]{1,0:T(8,128)}, u32[]{:S(2)}) copy-start(f32[24,512]{1,0:T(8,128)} %get-tuple-element.41) | copy-start | bytes 147460
  146.5 6.9 %copy-start.47 = (f32[24]{0:T(128)S(1)}, f32[24]{0:T(128)}, u32[]{:S(2)}) copy-start(f32[24]{0:T(128)} %param.20) | copy-start | bytes 292
  149.2 5.9 %copy-start.25 = (f32[512,128]{1,0:T(8,128)S(1)}, f32[512,128]{1,0:T(8,128)}, u32[]{:S(2)}) copy-start(f32[512,128]{1,0:T(8,128)} %get-tuple-element.43) | copy-start | bytes 786436
  149.2 5.9 %copy-start.24 = (f32[512,128]{1,0:T(8,128)S(1)}, f32[512,128]{1,0:T(8,128)}, u32[]{:S(2)}) copy-start(f32[512,128]{1,0:T(8,128)} %get-tuple-element.44) | copy-start | bytes 786436
  150.4 4.5 %copy-start.8 = (f32[512,1536]{1,0:T(8,128)S(1)}, f32[512,1536]{1,0:T(8,128)}, u32[]{:S(2)}) copy-start(f32[512,1536]{1,0:T(8,128)} %get-tuple-element.42) | copy-start | bytes 9437188
  169.6 3.5 %copy-start.14 = (bf16[2,2,2,2,2,24,1048]{6,5,0,2,3,1,4:T(8,128)(2,1)S(1)}, bf16[2,2,2,2,2,24,1048]{6,5,0,2,3,1,4:T(8,128)(2,1)}, u32[]{:S(2)}) copy-start(bf16[2,2,2,2,2,24,1048]{6,5,0,2,3,1,4:T(8,128)(2,1)} %copy-done.13) | copy-start | bytes 4829188
  169.7 3.5 %copy-start.35 = (f32[768]{0:T(1024)S(1)}, f32[768]{0:T(1024)}, u32[]{:S(2)}) copy-start(f32[768]{0:T(1024)} %copy-done.34) | copy-start | bytes 9220
  169.7 3.5 %copy-start.37 = (f32[512]{0:T(512)S(1)}, f32[512]{0:T(512)}, u32[]{:S(2)}) copy-start(f32[512]{0:T(512)} %copy-done.36) | copy-start | bytes 6148
  173.1 3.4 %copy-start.27 = (f32[7168]{0:T(1024)S(1)}, f32[7168]{0:T(1024)}, u32[]{:S(2)}) copy-start(f32[7168]{0:T(1024)} %reshape.302) | copy-start | bytes 86020
  173.1 3.4 %copy-start.29 = (f32[1792]{0:T(1024)S(1)}, f32[1792]{0:T(1024)}, u32[]{:S(2)}) copy-start(f32[1792]{0:T(1024)} %get-tuple-element.58) | copy-start | bytes 21508
  173.1 3.4 %copy-start.38 = (f32[1536]{0:T(1024)S(1)}, f32[1536]{0:T(1024)}, u32[]{:S(2)}) copy-start(f32[1536]{0:T(1024)} %get-tuple-element.56) | copy-start | bytes 18436
  173.2 3.4 %copy-start.40 = (f32[24]{0:T(128)S(1)}, f32[24]{0:T(128)}, u32[]{:S(2)}) copy-start(f32[24]{0:T(128)} %reduce_sum.146) | copy-start | bytes 292
  173.2 3.4 %copy-start.44 = (f32[24]{0:T(128)S(1)}, f32[24]{0:T(128)}, u32[]{:S(2)}) copy-start(f32[24]{0:T(128)} %get-tuple-element.66) | copy-start | bytes 292
  173.2 4.1 %copy-start.33 = (f32[512]{0:T(512)S(1)}, f32[512]{0:T(512)}, u32[]{:S(2)}) copy-start(f32[512]{0:T(512)} %copy-done.32) | copy-start | bytes 6148
  173.2 4.1 %copy-start.17 = (bf16[512,768]{1,0:T(8,128)(2,1)S(1)}, bf16[512,768]{1,0:T(8,128)(2,1)}, u32[]{:S(2)}) copy-start(bf16[512,768]{1,0:T(8,128)(2,1)} %param.13) | copy-start | bytes 2359300
  (18 other events, 43.7 us)
where the time goes:
time: 253 us; the launch traced here: 252 us
  Pallas kernels  139 us (55%)
  local copies, waits for them, and re-layouts  53.1 us (21%)
  other arithmetic  36.3 us (14%)
  matrix products  21.6 us (9%)
    pallas_call x1, Pallas kernels, reduce_all(): pl.pallas_call(functools.partial(reduce_kernel, plan, bits_of('rep')), in...  54.3 us
    pallas_call x1, Pallas kernels, gather_all(): pl.pallas_call(functools.partial(gather_kernel, plan), in_specs=[vmem] *...  50 us
    pallas_call x1, Pallas kernels, mixer_core(): mixed = span_scan(active, step, cum, jnp.repeat(skip_weight, HD)[None])  22.3 us
    pallas_call x1, Pallas kernels, span_scan(): pl.pallas_call(scan_fwd_kernel, grid=(NH // PAIR,), in_specs=scan_specs(l...  12.7 us
    dot_general x6, matrix products, contract(): lax.dot_general(left, right, (((left_dim,), (right_dim,)), ((), ())), pre...  12.6 us
    unnamed x101, local copies, waits for them, and re-layouts  10.5 us
    reshape x6, local copies, waits for them, and re-layouts, from_order(): split = blocks.reshape((2,) * len(labels) + blocks.shape[1:])  7.54 us
    reshape x6, local copies, waits for them, and re-layouts, to_order(): split = array.reshape((2,) * len(labels) + (rows, array.shape[1]))  7 us

commit v1 on v0

v1 whole, which is shorter than its diff:
```python
import functools


import jax
import jax.numpy as jnp
from jax import lax
from jax.experimental import pallas as pl
from jax.experimental.pallas import tpu as pltpu
from jax.sharding import PartitionSpec as P

NH = 24
HD = 64
NS = 128
KCONV = 4
DI = 1536
CONV_CH = 1792
PROJ = 3352
LANES = 128
PAIR = LANES // HD

EPS = 1e-05
HIGH = lax.Precision.HIGHEST


def contract(left, right, left_dim, right_dim, precision=None):
    return lax.dot_general(
        left,
        right,
        (((left_dim,), (right_dim,)), ((), ())),
        precision=precision,
        preferred_element_type=jnp.float32,
    )


LOG2E = 1.4426950408889634
QLEN = 128
GROUP = 3


def split_hi_lo(value):
    high = value.astype(jnp.bfloat16)
    return high, (value - high.astype(jnp.float32)).astype(jnp.bfloat16)


def row_loop(total, size, step):
    def one(i, carry):
        step(pl.multiple_of(i * size, size))
        return carry

    lax.fori_loop(0, total // size, one, 0)


def fold(value):
    return jnp.sum(value.reshape(-1, 8, value.shape[-1]), axis=0)


def head_expander(width):
    row = lax.broadcasted_iota(jnp.int32, (LANES, width), 0)
    col = lax.broadcasted_iota(jnp.int32, (LANES, width), 1)
    return jnp.where(row % HD == col // HD, 1.0, 0.0).astype(jnp.bfloat16)


def head_summer(width):
    row = lax.broadcasted_iota(jnp.int32, (width, LANES), 0)
    col = lax.broadcasted_iota(jnp.int32, (width, LANES), 1)
    return jnp.where(row // HD == col, 1.0, 0.0).astype(jnp.bfloat16)


def two_part(value):
    high = value.astype(jnp.bfloat16).astype(jnp.float32)
    low = pltpu.roll(value - high, HD, 1)
    lane = lax.broadcasted_iota(jnp.int32, value.shape, 1)
    return jnp.where(lane < HD, high, low).astype(jnp.bfloat16)


def stage_norm(r):
    total = r.hidden.shape[0]

    def step(at):
        rows = pl.ds(at, 64)
        h = r.hidden[rows, :].astype(jnp.float32)
        scale = lax.rsqrt(jnp.mean(h * h, axis=-1, keepdims=True) + EPS)
        r.nb[rows, :] = (h * scale * r.gain[...]).astype(jnp.bfloat16)

    row_loop(total, 64, step)
    r.nbt[...] = r.nb[...].T
    r.expand[...] = head_expander(DI)
    r.summer[...] = head_summer(DI)


def stage_proj_x(r, k):
    total = r.hidden.shape[0]
    width = r.wx[k].shape[1]
    r.raw[8 : 8 + total, k * width : (k + 1) * width] = contract(r.nb[...], r.wx[k][...], 1, 0)


def stage_conv(r):
    total = r.hidden.shape[0]
    r.raw[0:8, :] = jnp.zeros((8, r.raw.shape[1]), jnp.float32)
    size, wide = 64, 256

    def step(at):
        for lanes in range(0, CONV_CH, wide):
            cols = slice(lanes, lanes + wide)
            block = r.raw[pl.ds(at, size + 8), cols]
            conv = jnp.zeros((size, wide), jnp.float32) + r.cb[:, cols]
            for k in range(KCONV):
                start = 8 - (KCONV - 1) + k
                conv = conv + r.cw[k : k + 1, cols] * block[start : start + size]
            sig = jax.nn.sigmoid(conv)
            act = conv * sig
            r.act[pl.ds(at, size), cols] = act
            r.dsil[pl.ds(at, size), cols] = sig + act * (1.0 - sig)

    row_loop(total, size, step)


def stage_steps(r):
    total = r.hidden.shape[0]
    lane = lax.broadcasted_iota(jnp.int32, (1, LANES), 1)
    rate = jnp.where(lane < NH, jnp.exp(r.dl[...]), 0.0)
    row = lax.broadcasted_iota(jnp.int32, (QLEN, QLEN), 0)
    col = lax.broadcasted_iota(jnp.int32, (QLEN, QLEN), 1)
    lower = jnp.where(row >= col, 1.0, 0.0)

    def step(at):
        rows = pl.ds(at, QLEN)
        pre = r.raw[pl.ds(at + 8, QLEN), CONV_CH : CONV_CH + LANES] + r.sb[...]
        dt = jnp.maximum(pre, 0.0) + jnp.log1p(jnp.exp(-jnp.abs(pre)))
        dt = jnp.where(lane < NH, dt, 0.0)
        r.dt[rows, :] = dt
        r.sgd[rows, :] = jax.nn.sigmoid(pre)
        cum = contract(lower, -dt * rate, 1, 0, lax.Precision.HIGHEST) * LOG2E
        r.cum[rows, :] = cum
        r.cumt[rows, :] = cum.T

    row_loop(total, QLEN, step)


def chunk_factors(r, rows):
    cum = r.cum[rows, :]
    last = cum[QLEN - 1 : QLEN, :]
    stack = jnp.concatenate(
        [two_part(r.dt[rows, :]), two_part(jnp.exp2(cum)), two_part(jnp.exp2(last - cum))], axis=0
    )
    half = DI // 2
    for side in range(2):
        cols = slice(side * half, (side + 1) * half)
        r.ex[0 : 3 * QLEN, cols] = contract(stack, r.expand[:, cols], 1, 0)


def halves(value):
    lane = lax.broadcasted_iota(jnp.int32, value.shape, 1)
    zero = jnp.zeros_like(value)
    return jnp.concatenate(
        [jnp.where(lane < HD, value, zero), jnp.where(lane >= HD, value, zero)], axis=0
    )


def stage_scan(r):
    total = r.hidden.shape[0]
    row = lax.broadcasted_iota(jnp.int32, (QLEN, QLEN), 0)
    col = lax.broadcasted_iota(jnp.int32, (QLEN, QLEN), 1)
    r.state[...] = jnp.zeros_like(r.state)

    def step(at):
        rows = pl.ds(at, QLEN)
        keys = r.act[rows, DI : DI + NS]
        query = r.act[rows, DI + NS : DI + 2 * NS]
        score = jnp.where(row >= col, contract(query, keys, 1, 1, lax.Precision.HIGHEST), 0.0)
        query_b = query.astype(jnp.bfloat16)
        keys_t = keys.T.astype(jnp.bfloat16)
        chunk_factors(r, rows)
        r.states[rows, :] = r.state[...].astype(jnp.bfloat16)
        cum = r.cum[rows, :]
        cumt = r.cumt[rows, :]
        for p in range(NH // PAIR):
            cols = slice(p * LANES, (p + 1) * LANES)
            x = r.act[rows, cols]
            scaled_f = x * r.ex[0:QLEN, cols]
            scaled = scaled_f.astype(jnp.bfloat16)
            tail = (scaled_f * r.ex[2 * QLEN : 3 * QLEN, cols]).astype(jnp.bfloat16)
            parts = []
            for sub in range(PAIR):
                head = p * PAIR + sub
                spread = cum[:, head : head + 1] - cumt[head : head + 1, :]
                parts.append((score * jnp.exp2(jnp.minimum(spread, 0.0))).astype(jnp.bfloat16))
            inner = contract(jnp.concatenate(parts, axis=1), halves(scaled), 1, 0)
            lead = r.ex[QLEN : 2 * QLEN, cols]
            outer = contract(query_b, r.states[rows, cols], 1, 0)
            r.ysc[rows, cols] = inner + lead * outer
            r.state[:, cols] = lead[QLEN - 1 : QLEN, :] * r.state[:, cols] + contract(
                keys_t, tail, 1, 0
            )

    row_loop(total, QLEN, step)


def stage_proj_z(r, k):
    width = r.wz[k].shape[1]
    r.z[:, k * width : (k + 1) * width] = contract(r.nb[...], r.wz[k][...], 1, 0)


def stage_gate(r):
    total = r.hidden.shape[0]
    size = 16
    r.skx[...] = contract(two_part(jnp.broadcast_to(r.sk[...], (8, LANES))), r.expand[...], 1, 0)

    def step(at):
        rows = pl.ds(at, size)
        y = r.ysc[rows, :] + r.skx[0:1, :] * r.act[rows, 0:DI]
        z = r.z[rows, :]
        q = y * (z * jax.nn.sigmoid(z))
        scale = lax.rsqrt(jnp.mean(q * q, axis=-1, keepdims=True) + EPS)
        r.gb[rows, :] = (q * scale * r.mg[...]).astype(jnp.bfloat16)
        r.r2[rows, :] = jnp.broadcast_to(scale, (size, LANES))

    row_loop(total, size, step)


def live_rows(r, at, size):
    position = lax.broadcasted_iota(jnp.int32, (size, 1), 0) + at
    return jnp.where(position < r.count[0], 1.0, 0.0)


def stage_out(r):
    total, wide = r.hidden.shape

    def step(at):
        rows = pl.ds(at, 64)
        live = live_rows(r, at, 64)
        r.cl[rows, :] = (r.cot[rows, :].astype(jnp.float32) * live).astype(jnp.bfloat16)

    row_loop(total, 64, step)
    parts = len(r.wo)
    width = wide // parts
    for k in range(parts):
        cols = slice(k * width, (k + 1) * width)
        branch = contract(r.gb[...], r.wo[k][...], 1, 0)
        live = live_rows(r, 0, total)
        r.block_out[:, cols] = (r.hidden[:, cols].astype(jnp.float32) + live * branch).astype(
            jnp.bfloat16
        )
    block = 256
    for at in range(0, DI, block):
        sums = None
        for k in range(parts):
            cols = slice(k * width, (k + 1) * width)
            term = contract(r.cl[:, cols], r.wo[k][at : at + block, :], 1, 1)
            sums = term if sums is None else sums + term
        r.dy[:, at : at + block] = sums


def stage_grad_out(r, k):
    width = r.gwo[k].shape[1]
    part = contract(r.gb[...], r.cl[:, k * width : (k + 1) * width], 0, 0)
    r.gwo[k][...] = part.astype(jnp.bfloat16)


def stage_gate_back(r):
    total = r.hidden.shape[0]
    size = 16
    r.acc_mg[...] = jnp.zeros_like(r.acc_mg)
    r.acc_sk[...] = jnp.zeros_like(r.acc_sk)

    def step(at):
        rows = pl.ds(at, size)
        x = r.act[rows, 0:DI]
        y = r.ysc[rows, :] + r.skx[0:1, :] * x
        z = r.z[rows, :]
        sig = jax.nn.sigmoid(z)
        gate = z * sig
        q = y * gate
        scale = r.r2[rows, 0:1]
        dg = r.dy[rows, :]
        r.acc_mg[...] += fold(dg * q * scale)
        dn = dg * r.mg[...]
        mean = jnp.sum(dn * q, axis=-1, keepdims=True) * (1.0 / DI)
        dq = scale * (dn - q * (scale * scale * mean))
        dy = dq * gate
        r.dy[rows, :] = dy
        r.acc_sk[...] += fold(dy * x)
        r.dz[rows, :] = (dq * y * (sig + gate * (1.0 - sig))).astype(jnp.bfloat16)

    row_loop(total, size, step)


def stage_grad_z(r, k):
    width = r.gwz[k].shape[1]
    part = contract(r.nbt[...], r.dz[:, k * width : (k + 1) * width], 1, 0)
    r.gwz[k][...] = part.astype(jnp.bfloat16)


def head_sums(r, values):
    parts = []
    for value in values:
        parts += list(split_hi_lo(value))
    sums = contract(jnp.concatenate(parts, axis=0), r.summer[...], 1, 0)
    out, at = [], 0
    for value in values:
        count = value.shape[0]
        out.append(sums[at : at + count] + sums[at + count : at + 2 * count])
        at += 2 * count
    return out


def stage_scan_back(r):
    total = r.hidden.shape[0]
    chunks = total // QLEN
    row = lax.broadcasted_iota(jnp.int32, (QLEN, QLEN), 0)
    col = lax.broadcasted_iota(jnp.int32, (QLEN, QLEN), 1)
    upper = jnp.where(col >= row, 1.0, 0.0)
    lane = lax.broadcasted_iota(jnp.int32, (1, LANES), 1)
    rate = jnp.where(lane < NH, jnp.exp(r.dl[...]), 0.0)
    r.dstate[...] = jnp.zeros_like(r.dstate)
    r.acc_dl[...] = jnp.zeros_like(r.acc_dl)
    r.acc_sb[...] = jnp.zeros_like(r.acc_sb)

    def step(i, carry):
        at = pl.multiple_of((chunks - 1 - i) * QLEN, QLEN)
        rows = pl.ds(at, QLEN)
        keys = r.act[rows, DI : DI + NS]
        query = r.act[rows, DI + NS : DI + 2 * NS]
        score = jnp.where(col >= row, contract(keys, query, 1, 1, lax.Precision.HIGHEST), 0.0)
        keys_b = keys.astype(jnp.bfloat16)
        query_t = query.T.astype(jnp.bfloat16)
        chunk_factors(r, rows)
        cum = r.cum[rows, :]
        cumt = r.cumt[rows, :]
        r.dscore[...] = jnp.zeros_like(r.dscore)
        r.dkq[...] = jnp.zeros_like(r.dkq)
        for p in range(NH // PAIR):
            cols = slice(p * LANES, (p + 1) * LANES)
            dy = r.dy[rows, cols]
            dy_b = dy.astype(jnp.bfloat16)
            x = r.act[rows, cols]
            scaled_f = x * r.ex[0:QLEN, cols]
            scaled = scaled_f.astype(jnp.bfloat16)
            tail = (scaled_f * r.ex[2 * QLEN : 3 * QLEN, cols]).astype(jnp.bfloat16)
            lead = r.ex[QLEN : 2 * QLEN, cols]
            stacked = halves(dy_b)
            d_mixed = contract(scaled, stacked, 1, 1)
            parts = []
            gain = None
            for sub in range(PAIR):
                head = p * PAIR + sub
                spread = cumt[head : head + 1, :] - cum[:, head : head + 1]
                decay = jnp.exp2(jnp.minimum(spread, 0.0))
                term = d_mixed[:, sub * QLEN : (sub + 1) * QLEN] * decay
                gain = term if gain is None else gain + term
                parts.append((score * decay).astype(jnp.bfloat16))
            r.dscore[...] += gain
            d_state = r.dstate[:, cols]
            d_state_b = d_state.astype(jnp.bfloat16)
            d_scaled = contract(jnp.concatenate(parts, axis=1), stacked, 1, 0)
            d_outer = r.ex[2 * QLEN : 3 * QLEN, cols] * contract(keys_b, d_state_b, 1, 0)
            d_scaled = d_scaled + d_outer
            dy_lead = (dy * lead).astype(jnp.bfloat16)
            r.dkq[:, 0:NS] += contract(tail, d_state_b, 1, 1)
            r.dkq[:, NS : 2 * NS] += contract(dy_lead, r.states[rows, cols], 1, 1)
            kept = lead[QLEN - 1 : QLEN, :] * r.states[rows, cols].astype(jnp.float32)
            across = kept * d_state + scaled.astype(jnp.float32) * d_outer
            r.zrow[0:1, cols] = jnp.sum(across, axis=0, keepdims=True)
            r.dstate[:, cols] = lead[QLEN - 1 : QLEN, :] * d_state + contract(
                query_t, dy_lead, 1, 0
            )
            r.prod[0:QLEN, cols] = (
                dy_b.astype(jnp.float32) * r.ysc[rows, cols]
                - scaled.astype(jnp.float32) * d_scaled
            )
            r.prod[QLEN : 2 * QLEN, cols] = x * d_scaled
            dx = d_scaled * r.ex[0:QLEN, cols] + r.skx[0:1, cols] * dy
            r.act[rows, cols] = dx * r.dsil[rows, cols]
        dscore = jnp.where(col >= row, r.dscore[...], 0.0)
        d_keys = contract(dscore, query, 1, 0, lax.Precision.HIGHEST) + r.dkq[:, 0:NS]
        d_query = contract(dscore.T, keys, 1, 0, lax.Precision.HIGHEST) + r.dkq[:, NS : 2 * NS]
        both = jnp.concatenate([d_keys, d_query], axis=1)
        r.act[rows, DI:CONV_CH] = both * r.dsil[rows, DI:CONV_CH]
        flow, d_dt, across = head_sums(
            r, [r.prod[0:QLEN, :], r.prod[QLEN : 2 * QLEN, :], jnp.broadcast_to(r.zrow[0:1, :], (16, DI))]
        )
        da = contract(upper, flow, 1, 0, lax.Precision.HIGHEST) + across[0:1, :]
        dt = r.dt[rows, :]
        r.acc_dl[...] += fold(-da * dt * rate)
        d_pre = (d_dt - da * rate) * r.sgd[rows, :]
        d_pre = jnp.where(lane < NH, d_pre, 0.0)
        r.acc_sb[...] += fold(d_pre)
        r.dxb[rows, CONV_CH : CONV_CH + LANES] = d_pre.astype(jnp.bfloat16)
        return carry

    lax.fori_loop(0, chunks, step, 0)


def stage_conv_back(r):
    total = r.hidden.shape[0]
    size, wide = 64, 256
    r.act[total : total + 8, :] = jnp.zeros((8, CONV_CH), jnp.float32)
    r.acc_cw[...] = jnp.zeros_like(r.acc_cw)

    def step(at):
        for lanes in range(0, CONV_CH, wide):
            cols = slice(lanes, lanes + wide)
            grads = r.act[pl.ds(at, size + 8), cols]
            inputs = r.raw[pl.ds(at, size + 8), cols]
            here = grads[0:size]
            total_in = None
            for k in range(KCONV):
                shift = KCONV - 1 - k
                term = r.cw[k : k + 1, cols] * grads[shift : shift + size]
                total_in = term if total_in is None else total_in + term
                start = 8 - (KCONV - 1) + k
                r.acc_cw[k * 8 : (k + 1) * 8, cols] += fold(here * inputs[start : start + size])
            r.acc_cw[KCONV * 8 : (KCONV + 1) * 8, cols] += fold(here)
            r.dxb[pl.ds(at, size), cols] = total_in.astype(jnp.bfloat16)

    row_loop(total, size, step)


def stage_grad_x(r, k):
    width = r.gwx[k].shape[1]
    part = contract(r.nbt[...], r.dxb[:, k * width : (k + 1) * width], 1, 0)
    r.gwx[k][...] = part.astype(jnp.bfloat16)


def stage_grad_in(r):
    total, wide = r.hidden.shape
    block = 256
    for at in range(0, wide, block):
        sums = None
        for grads, weights in ((r.dz, r.wz), (r.dxb, r.wx)):
            width = weights[0].shape[1]
            for k in range(len(weights)):
                term = contract(
                    grads[:, k * width : (k + 1) * width], weights[k][at : at + block, :], 1, 1
                )
                sums = term if sums is None else sums + term
        r.grad_in[:, at : at + block] = sums


def stage_norm_back(r):
    total, wide = r.hidden.shape
    r.acc_gain[...] = jnp.zeros_like(r.acc_gain)

    def step(at):
        rows = pl.ds(at, 32)
        h = r.hidden[rows, :].astype(jnp.float32)
        scale = lax.rsqrt(jnp.mean(h * h, axis=-1, keepdims=True) + EPS)
        dn = r.grad_in[rows, :]
        r.acc_gain[...] += fold(dn * (h * scale))
        dn = dn * r.gain[...]
        mean = jnp.sum(dn * h, axis=-1, keepdims=True) * (1.0 / wide)
        r.grad_in[rows, :] = r.cot[rows, :].astype(jnp.float32) + scale * (
            dn - h * (scale * scale * mean)
        )

    row_loop(total, 32, step)


def stage_vectors(r):
    r.vec[...] = jnp.zeros_like(r.vec)
    for k in range(KCONV + 1):
        r.vec[k : k + 1, :] = jnp.sum(r.acc_cw[k * 8 : (k + 1) * 8, :], axis=0, keepdims=True)
    r.vec[5:6, 0:DI] = jnp.sum(r.acc_mg[...], axis=0, keepdims=True)
    wide = r.acc_gain.shape[1]
    r.vec[6:7, 0:wide] = jnp.sum(r.acc_gain[...], axis=0, keepdims=True)
    r.vec[7:8, 0:LANES] = jnp.sum(r.acc_sb[...], axis=0, keepdims=True)
    r.vec[7:8, LANES : 2 * LANES] = jnp.sum(r.acc_dl[...], axis=0, keepdims=True)
    sums = jnp.sum(r.acc_sk[...], axis=0, keepdims=True)
    (heads,) = head_sums(r, [jnp.broadcast_to(sums, (16, DI))])
    r.vec[7:8, 2 * LANES : 3 * LANES] = heads[0:1, :]


class Refs:
    pass


def core_scratch(total, wide):
    f32, bf16 = jnp.float32, jnp.bfloat16
    span = CONV_CH + LANES
    return dict(
        nb=((total, wide), bf16),
        nbt=((wide, total), bf16),
        expand=((LANES, DI), bf16),
        summer=((DI, LANES), bf16),
        raw=((total + 8, span), f32),
        act=((total + 8, CONV_CH), f32),
        dsil=((total, CONV_CH), f32),
        dt=((total, LANES), f32),
        sgd=((total, LANES), f32),
        cum=((total, LANES), f32),
        cumt=((total, LANES), f32),
        state=((NS, DI), f32),
        dstate=((NS, DI), f32),
        states=((total, DI), bf16),
        ysc=((total, DI), f32),
        z=((total, DI), f32),
        skx=((8, DI), f32),
        gb=((total, DI), bf16),
        r2=((total, LANES), f32),
        cl=((total, wide), bf16),
        dy=((total, DI), f32),
        dz=((total, DI), bf16),
        dxb=((total, span), bf16),
        dscore=((QLEN, QLEN), f32),
        dkq=((QLEN, 2 * NS), f32),
        zrow=((8, DI), f32),
        prod=((2 * QLEN, DI), f32),
        acc_mg=((8, DI), f32),
        acc_sk=((8, DI), f32),
        acc_dl=((8, LANES), f32),
        acc_sb=((8, LANES), f32),
        acc_cw=((8 * (KCONV + 1), CONV_CH), f32),
        acc_gain=((8, wide), f32),
    )


def bits_of(axis):
    size = lax.axis_size(axis)
    return [(axis, 1 << k) for k in reversed(range(size.bit_length() - 1))]


def all_labels():
    return bits_of("fsdp") + bits_of("rep")


def my_bit(label):
    return (lax.axis_index(label[0]) // label[1]) % 2


def partner(label):
    ids = {name: lax.axis_index(name) for name in ("fsdp", "rep")}
    ids[label[0]] = ids[label[0]] + label[1] * (1 - 2 * my_bit(label))
    return (ids["fsdp"], ids["rep"])


def greet(labels):
    barrier = pltpu.get_barrier_semaphore()
    for label in labels:
        pl.semaphore_signal(
            barrier, inc=1, device_id=partner(label), device_id_type=pl.DeviceIdType.MESH
        )
    pl.semaphore_wait(barrier, len(labels))


def send(source, target, sems, stream, slot, label):
    copy = pltpu.make_async_remote_copy(
        src_ref=source,
        dst_ref=target,
        send_sem=sems[0].at[stream, slot],
        recv_sem=sems[1].at[stream, slot],
        device_id=partner(label),
        device_id_type=pl.DeviceIdType.MESH,
    )
    copy.start()
    return copy


def orders():
    fsdp, rep = bits_of("fsdp"), bits_of("rep")
    near, wide = fsdp[-1:], fsdp[:-1]
    mid, far = wide[-1:], wide[:-1]
    core, row = rep[-1:], rep[:-1]
    return (
        core + row + near + mid + far,
        core + near + mid + row + far,
        core + mid + row + near + far,
    )


def position(order):
    place = 0
    for label in order:
        place = place * 2 + my_bit(label)
    return place


def gather_kernel(plan, *refs):
    count = len(plan)
    ins, outs = refs[:count], refs[count : 2 * count]
    sems, local = refs[2 * count : 2 * count + 2], refs[2 * count + 2]
    greet(all_labels())
    steps = max(len(order) for order in plan)
    open_sends, waiting, locals_ = [], {}, []
    for k in range(count):
        copy = pltpu.make_async_copy(ins[k], outs[k].at[pl.ds(position(plan[k]), 1)], local.at[k])
        copy.start()
        locals_.append(copy)
    for step in range(steps):
        for k, order in enumerate(plan):
            if step >= len(order):
                continue
            size = 1 << step
            start = position(order) // size * size
            if step == 0:
                source = ins[k]
            else:
                if step == 1:
                    locals_[k].wait()
                waiting[k].wait_recv()
                source = outs[k].at[pl.ds(start, size)]
            label = order[len(order) - 1 - step]
            copy = send(source, outs[k].at[pl.ds(start, size)], sems, k, step, label)
            waiting[k] = copy
            open_sends.append(copy)
    for k in range(count):
        waiting[k].wait_recv()
        if len(plan[k]) < 2:
            locals_[k].wait()
    for copy in open_sends:
        copy.wait_send()


def gather_all(plan, pieces):
    steps = max(len(order) for order in plan)
    vmem = pl.BlockSpec(memory_space=pltpu.VMEM)
    return pl.pallas_call(
        functools.partial(gather_kernel, plan),
        in_specs=[vmem] * len(pieces),
        out_specs=[vmem] * len(pieces),
        out_shape=[
            jax.ShapeDtypeStruct((1 << len(order),) + piece.shape[1:], piece.dtype)
            for order, piece in zip(plan, pieces)
        ],
        scratch_shapes=[
            pltpu.SemaphoreType.DMA((len(pieces), steps)),
            pltpu.SemaphoreType.DMA((len(pieces), steps)),
            pltpu.SemaphoreType.DMA((len(pieces),)),
        ],
        compiler_params=pltpu.CompilerParams(
            collective_id=0, has_side_effects=True, vmem_limit_bytes=60 << 20
        ),
        name="gather_weights",
    )(*pieces)


def reduce_kernel(plan, tail, *refs):
    count = len(plan)
    steps = len(plan[0])
    grads, vector = refs[:count], refs[count]
    outs, total = refs[count + 1 : 2 * count + 1], refs[2 * count + 1]
    at = 2 * count + 2
    held = [refs[at + k * steps : at + (k + 1) * steps] for k in range(count)]
    at += count * steps
    sums = refs[at : at + steps]
    sems, local = refs[at + steps : at + steps + 2], refs[at + steps + 2]
    labels = all_labels()
    greet(labels)
    open_sends, waiting = [], {}
    vector_order = labels[::-1]

    def source_of(k, step):
        return grads[k] if step == 0 else held[k][step - 1]

    def add_in(k, step):
        size = 1 << (steps - 1 - step)
        base = source_of(k, step)
        target = held[k][step]
        start = my_bit(plan[k][step]) * size

        def one(i, carry):
            left = base[start + i].astype(jnp.float32)
            target[i] = (left + target[i].astype(jnp.float32)).astype(target.dtype)
            return carry

        lax.fori_loop(0, size, one, 0)

    for step in range(steps):
        for k in range(count):
            if step > 0:
                waiting[k].wait_recv()
                add_in(k, step - 1)
            label = plan[k][step]
            size = 1 << (steps - 1 - step)
            away = source_of(k, step).at[pl.ds((1 - my_bit(label)) * size, size)]
            waiting[k] = send(away, held[k][step], sems, k, step, label)
            open_sends.append(waiting[k])
        if step > 0:
            waiting[count].wait_recv()
            before = vector if step == 1 else sums[step - 2]
            sums[step - 1][...] = before[...] + sums[step - 1][...]
        now = vector if step == 0 else sums[step - 1]
        waiting[count] = send(now, sums[step], sems, count, step, vector_order[step])
        open_sends.append(waiting[count])

    here = lax.axis_index("rep")
    known = {k: [0] for k in range(count)}
    inbox = {k: [] for k in range(count)}
    for hop, label in enumerate(tail):
        for k in range(count):
            if hop == 0:
                waiting[k].wait_recv()
                add_in(k, steps - 1)
                copy = pltpu.make_async_copy(
                    held[k][steps - 1], outs[k].at[pl.ds(here, 1)], local.at[k]
                )
                copy.start()
                waiting[k] = copy
            for copy in inbox[k]:
                copy.wait_recv()
            inbox[k] = []
            shift = label[1] * (1 - 2 * my_bit(label))
            for n, offset in enumerate(list(known[k])):
                place = pl.ds(here + offset, 1)
                source = held[k][steps - 1] if n == 0 else outs[k].at[place]
                copy = send(source, outs[k].at[place], sems, k, steps + (1 << hop) - 1 + n, label)
                inbox[k].append(copy)
                open_sends.append(copy)
                known[k].append(offset + shift)
    waiting[count].wait_recv()
    before = sums[steps - 2]
    total[...] = before[...] + sums[steps - 1][...]
    for k in range(count):
        for copy in inbox[k]:
            copy.wait_recv()
        waiting[k].wait()
    for copy in open_sends:
        copy.wait_send()


def reduce_all(plan, grads, vector):
    steps = len(plan[0])
    reps = lax.axis_size("rep")
    vmem = pl.BlockSpec(memory_space=pltpu.VMEM)
    slots = pltpu.SemaphoreType.DMA((len(grads) + 1, steps + reps))
    scratch = []
    for grad in grads:
        scratch += [
            pltpu.VMEM((1 << (steps - 1 - step),) + grad.shape[1:], grad.dtype)
            for step in range(steps)
        ]
    scratch += [pltpu.VMEM(vector.shape, vector.dtype) for _ in range(steps)]
    return pl.pallas_call(
        functools.partial(reduce_kernel, plan, bits_of("rep")),
        in_specs=[vmem] * (len(grads) + 1),
        out_specs=[vmem] * (len(grads) + 1),
        out_shape=[jax.ShapeDtypeStruct((reps,) + g.shape[1:], g.dtype) for g in grads]
        + [jax.ShapeDtypeStruct(vector.shape, vector.dtype)],
        scratch_shapes=scratch + [slots, slots, pltpu.SemaphoreType.DMA((len(grads),))],
        compiler_params=pltpu.CompilerParams(
            collective_id=1, has_side_effects=True, vmem_limit_bytes=60 << 20
        ),
        name="reduce_grads",
    )(*grads, vector)


def to_order(array, order):
    labels = all_labels()
    rows = array.shape[0] >> len(labels)
    perm = [labels.index(label) for label in order] + [len(labels), len(labels) + 1]
    split = array.reshape((2,) * len(labels) + (rows, array.shape[1]))
    return split.transpose(perm).reshape((-1, rows, array.shape[1]))


def from_order(blocks, order):
    labels = all_labels()
    perm = [order.index(label) for label in labels] + [len(labels), len(labels) + 1]
    split = blocks.reshape((2,) * len(labels) + blocks.shape[1:])
    return split.transpose(perm).reshape((-1, blocks.shape[-1]))


def whole_lanes(array):
    return jnp.pad(array, ((0, 0), (0, -array.shape[1] % LANES)))


def my_rows(shard):
    count = shard.shape[0] // lax.axis_size("rep")
    return lax.dynamic_slice_in_dim(shard, lax.axis_index("rep") * count, count, 0)


SMALL = ("gain", "cw", "cb", "sb", "dl", "sk", "mg")


def core_kernel(names, *refs):
    r = Refs()
    at = 0
    for name, many in names:
        if many:
            setattr(r, name, list(refs[at : at + many]))
            at += many
        else:
            setattr(r, name, refs[at])
            at += 1
    r.ex = r.z
    stage_norm(r)
    for k in range(GROUP):
        stage_proj_x(r, k)
    stage_conv(r)
    stage_steps(r)
    stage_scan(r)
    for k in range(GROUP):
        stage_proj_z(r, k)
    stage_gate(r)
    stage_out(r)
    for k in range(GROUP):
        stage_grad_out(r, k)
    stage_gate_back(r)
    for k in range(GROUP):
        stage_grad_z(r, k)
    stage_scan_back(r)
    stage_conv_back(r)
    for k in range(GROUP):
        stage_grad_x(r, k)
    stage_grad_in(r)
    stage_norm_back(r)
    stage_vectors(r)


def run_core(count, hidden, cot, small, wx, wz, wo):
    total, wide = hidden.shape
    f32, bf16 = jnp.float32, jnp.bfloat16
    scratch = core_scratch(total, wide)
    vmem = pl.BlockSpec(memory_space=pltpu.VMEM)
    smem = pl.BlockSpec(memory_space=pltpu.SMEM)
    outs = [((total, wide), bf16), ((total, wide), f32), ((8, CONV_CH), f32)]
    outs += [(w.shape, bf16) for w in wx + wz + wo]
    names = [("count", 0), ("hidden", 0), ("cot", 0)] + [(name, 0) for name in SMALL]
    names += [("wx", GROUP), ("wz", GROUP), ("wo", GROUP)]
    names += [("block_out", 0), ("grad_in", 0), ("vec", 0)]
    names += [("gwx", GROUP), ("gwz", GROUP), ("gwo", GROUP)]
    names += [(name, 0) for name in scratch]
    inputs = [count, hidden, cot] + [small[name] for name in SMALL] + wx + wz + wo
    return pl.pallas_call(
        functools.partial(core_kernel, names),
        in_specs=[smem] + [vmem] * (len(inputs) - 1),
        out_specs=[vmem] * len(outs),
        out_shape=[jax.ShapeDtypeStruct(*out) for out in outs],
        scratch_shapes=[pltpu.VMEM(*item) for item in scratch.values()],
        compiler_params=pltpu.CompilerParams(vmem_limit_bytes=67043328),
        name="mixer_block",
    )(*inputs)


def lane_row(array):
    return jnp.pad(array, (0, LANES - array.shape[0])).reshape(1, LANES)


def cuts_of():
    wide = -(-(CONV_CH + NH) // (GROUP * LANES)) * LANES
    x_cuts = [slice(DI + k * wide, min(DI + (k + 1) * wide, PROJ)) for k in range(GROUP)]
    z_cuts = [slice(k * DI // GROUP, (k + 1) * DI // GROUP) for k in range(GROUP)]
    return x_cuts, z_cuts


def body(
    hidden_in, cotangent, lengths, norm_gain, in_weight, conv_weight, conv_bias,
    step_bias, decay_log, skip_weight, mix_gain, out_weight,
):
    assert lengths.shape[0] == 1 and hidden_in.shape[0] % QLEN == 0
    plan = orders()
    x_cuts, z_cuts = cuts_of()
    width = out_weight.shape[1] // GROUP
    out_columns = [slice(k * width, (k + 1) * width) for k in range(GROUP)]
    small = jnp.concatenate([norm_gain, conv_weight.reshape(-1), conv_bias, mix_gain])
    small = jnp.pad(small, (0, -small.size % 2048)).reshape(1, -1, LANES)
    in_rows, out_rows = my_rows(in_weight), my_rows(out_weight)
    pieces = [whole_lanes(in_rows[:, cut])[None] for cut in x_cuts + z_cuts]
    pieces += [out_rows[None, :, cut] for cut in out_columns]
    wide_plan = list(plan) * 3
    gathered = gather_all([bits_of("fsdp")] + wide_plan, [small] + pieces)
    full = [from_order(blocks, order) for blocks, order in zip(gathered[1:], wide_plan)]
    small = gathered[0].reshape(lax.axis_size("fsdp"), -1)
    groups = small.shape[0]
    ends = [norm_gain.size, conv_weight.size, conv_bias.size]
    cut_a, cut_b, cut_c = ends[0], ends[0] + ends[1], sum(ends)
    f32 = jnp.float32
    params = dict(
        gain=small[:, :cut_a].reshape(1, -1).astype(f32),
        cw=small[:, cut_a:cut_b]
        .reshape(groups, KCONV, -1)
        .transpose(1, 0, 2)
        .reshape(KCONV, -1)
        .astype(f32),
        cb=small[:, cut_b:cut_c].reshape(1, -1).astype(f32),
        mg=small[:, cut_c : cut_c + mix_gain.size].reshape(1, -1).astype(f32),
        sb=lane_row(step_bias),
        dl=lane_row(decay_log),
        sk=lane_row(skip_weight),
    )
    block_out, grad_in, vec, *grads = run_core(
        lengths, hidden_in, cotangent, params, full[:3], full[3:6], full[6:]
    )
    blocks = [to_order(part, order) for part, order in zip(grads, wide_plan)]
    *sums, vec = reduce_all(wide_plan, blocks, vec)
    sums = [part.reshape(-1, part.shape[-1]) for part in sums]
    g_in = jnp.concatenate(sums[3:6] + sums[:3], axis=1)[:, :PROJ].astype(f32)
    g_out = jnp.concatenate(sums[6:], axis=1).astype(f32)
    me = lax.axis_index("fsdp")

    def mine(array):
        count = array.shape[-1] // groups
        return lax.dynamic_slice_in_dim(array, me * count, count, array.ndim - 1)

    g_cw = mine(vec[:KCONV])
    g_cb = mine(vec[KCONV])
    g_mg = mine(vec[5, :DI])
    g_gain = mine(vec[6, : hidden_in.shape[1]])
    g_sb, g_dl, g_sk = (vec[7, k * LANES : k * LANES + NH] for k in range(3))
    return (block_out, grad_in, g_gain, g_in, g_cw, g_cb, g_sb, g_dl, g_sk, g_mg, g_out)


def solution(mesh):
    in_specs = (
        P(("fsdp", "rep"), None),
        P(("fsdp", "rep"), None),
        P(("fsdp", "rep")),
        P("fsdp"),
        P("fsdp", None),
        P(None, "fsdp"),
        P("fsdp"),
        P(),
        P(),
        P(),
        P("fsdp"),
        P("fsdp", None),
    )
    out_specs = (
        P(("fsdp", "rep"), None),
        P(("fsdp", "rep"), None),
        P("fsdp"),
        P("fsdp", None),
        P(None, "fsdp"),
        P("fsdp"),
        P(),
        P(),
        P(),
        P("fsdp"),
        P("fsdp", None),
    )
    return jax.shard_map(body, mesh=mesh, in_specs=in_specs, out_specs=out_specs, check_vma=False)
```

time: 253 us -> 210 us (0.83)
  other arithmetic: 36.3 us -> 3.28 us
  Pallas kernels: 139 us -> 165 us
  matrix products: 21.6 us -> 0 us
  local copies, waits for them, and re-layouts: 53.1 us -> 39.8 us
    pallas_call x2 -> x1, Pallas kernels: 35 us -> 64.7 us  [run_core(): pl.pallas_call(functools.partial(core_kernel, names), in_specs=[smem] + [...]
    dot_general x10 -> x0, matrix products: 21.6 us -> none  [the longest x6 12.6 us: contract(): lax.dot_general(left, right, (((left_dim,), (right_dim,)), ((), ())), pre...]
    mul x4 -> x0, other arithmetic: 13.4 us -> none  [the longest x1 5.45 us: mixer_core(): flat = mixed * jax.nn.silu(gate)]
    reduce_sum x4 -> x0, other arithmetic: 12.5 us -> none  [the longest x1 6.51 us: mixer_core(): conv_out = conv_out + conv_w[offset] * padded[offset:offset + length]]
    slice x10 -> x5, local copies, waits for them, and re-layouts: 8.45 us -> 0.79 us  [the longest x1 0.76 us: body(): pieces = [whole_lanes(in_rows[:, cut])[None] for cut in x_cuts + z_cuts]]
    unnamed x101 -> x54, local copies, waits for them, and re-layouts: 10.5 us -> 3.76 us
    convert_element_type x8 -> x6, other arithmetic: 7.39 us -> 3.28 us  [the longest x1 1.9 us: body(): g_out = jnp.concatenate(sums[6:], axis=1).astype(f32)]
    reshape x6 -> x9, local copies, waits for them, and re-layouts: 7 us -> 10.4 us  [to_order(): split = array.reshape((2,) * len(labels) + (rows, array.shape[1]))]
where the time goes in v1:
time: 210 us; the launch traced here: 209 us
  Pallas kernels  165 us (79%)
  local copies, waits for them, and re-layouts  39.8 us (19%)
  other arithmetic  3.28 us (2%)
    pallas_call x1, Pallas kernels, run_core(): pl.pallas_call(functools.partial(core_kernel, names), in_specs=[smem] + [...  64.7 us
    pallas_call x1, Pallas kernels, reduce_all(): pl.pallas_call(functools.partial(reduce_kernel, plan, bits_of('rep')), in...  52.4 us
    pallas_call x1, Pallas kernels, gather_all(): pl.pallas_call(functools.partial(gather_kernel, plan), in_specs=[vmem] *...  47.6 us
    reshape x9, local copies, waits for them, and re-layouts, to_order(): split = array.reshape((2,) * len(labels) + (rows, array.shape[1]))  10.4 us
    reshape x9, local copies, waits for them, and re-layouts, from_order(): split = blocks.reshape((2,) * len(labels) + blocks.shape[1:])  10.3 us

profile of v1, /device:TPU:0, one launch (start us, length us, event | category | flops | bytes accessed | tf_op | source)
XLA Modules:
  0.0 209.2 jit_solution(13526320682661106238)
XLA Ops:
  0.6 0.8 dynamic-slice.5
  1.4 1.4 dynamic-slice_bitcast_fusion
  2.8 1.4 dynamic-slice_bitcast_fusion.5
  4.2 1.4 dynamic-slice_bitcast_fusion.2
  5.6 0.8 reshape.229
  6.4 2.1 concatenate.9
  9.1 47.6 %gather_weights.1 = (bf16[8,16,128]{2,1,0:T(8,128)(2,1)}, bf16[32,24,640]{2,1,0:T(8,128)(2,1)}, bf16[32,24,640]{2,1,0:T(8,128)(2,1)}, bf16[32,24,640]{2,1,0:T(8,...) custom-call(bf16[1,16,128]{2,1,0:T(8,128)(2,1)} %pad_bitcast_fusion., ...), custom_call_target="tpu_custom_call" | custom-call | tf_op jit(solution)/shard_map/gather_weights/pallas_call | solution.py:616
  56.6 0.9 copy.45
  60.5 2.2 %copy.24 = bf16[2,2,2,2,2,24,640]{6,5,0,1,2,3,4:T(8,128)(2,1)} copy(bf16[2,2,2,2,2,24,640]{6,5,4,3,2,1,0:T(8,128)(2,1)} %bitcast.144) | data formatting | bytes 1966080 | tf_op jit(solution)/shard_map/reshape | solution.py:757
  62.8 1.1 copy.25
  64.3 1.0 copy.26
  65.4 1.0 copy.27
  66.4 1.1 copy.28
  67.4 1.0 copy.29
  68.4 1.0 copy.30
  69.4 1.0 copy.31
  70.4 1.0 copy.32
  73.1 64.7 %mixer_block.1 = (bf16[512,768]{1,0:T(8,128)(2,1)}, f32[512,768]{1,0:T(8,128)}, f32[8,1792]{1,0:T(8,128)}, bf16[768,640]{1,0:T(8,128)(2,1)}, bf16[768,640]{1,0:T...) custom-call(s32[1]{0:T(128)S(6)} %copy.52.refs_0_, ...), custom_call_target="tpu_custom_call" | custom-call | tf_op jit(solution)/shard_map/mixer_block/pallas_call | solution.py:822
  137.8 2.3 %copy.33 = bf16[2,2,2,2,2,24,640]{6,5,0,1,2,3,4:T(8,128)(2,1)} copy(bf16[2,2,2,2,2,24,640]{6,5,4,3,2,1,0:T(8,128)(2,1)} %bitcast.147) | data formatting | bytes 1966080 | tf_op jit(solution)/shard_map/reshape | solution.py:750
  140.1 1.1 copy.34
  141.7 1.0 copy.35
  142.7 1.0 copy.36
  143.7 1.1 copy.37
  144.8 1.0 copy.38
  145.8 1.0 copy.39
  146.8 1.0 copy.40
  147.8 1.0 copy.41
  148.7 52.4 %reduce_grads.1 = (bf16[4,24,640]{2,1,0:T(8,128)(2,1)}, bf16[4,24,640]{2,1,0:T(8,128)(2,1)}, bf16[4,24,640]{2,1,0:T(8,128)(2,1)}, bf16[4,24,512]{2,1,0:T(8,128)(...) custom-call(bf16[32,24,640]{2,1,0:T(8,128)(2,1)} %bitcast.124, ...), custom_call_target="tpu_custom_call" | custom-call | tf_op jit(solution)/shard_map/reduce_grads/pallas_call | solution.py:732
  201.1 1.9 maximum_convert_fusion
  203.1 0.9 constant_dynamic-update-slice_fusion.5
  204.0 0.9 constant_dynamic-update-slice_fusion.4
  205.0 1.1 slice_convert_fusion
  (74 shorter events, 8.9 us)
Async XLA Ops:
  56.6 6.1 %copy-start.1 = (bf16[32,24,640]{2,1,0:T(8,128)(2,1)S(1)}, bf16[32,24,640]{2,1,0:T(8,128)(2,1)}, u32[]{:S(2)}) copy-start(bf16[32,24,640]{2,1,0:T(8,128)(2,1)} %get-tuple-element.45) | copy-start | bytes 2949124
  62.8 1.6 copy-start
  63.8 1.5 copy-start.9
  64.3 2.0 copy-start.8
  65.4 2.1 copy-start.7
  66.4 2.1 copy-start.6
  67.4 2.0 copy-start.5
  68.4 2.0 copy-start.4
  69.4 2.0 copy-start.21
  69.4 2.0 copy-start.22
  69.4 3.1 %copy-start.23 = (f32[24]{0:T(128)S(1)}, f32[24]{0:T(128)}, u32[]{:S(2)}) copy-start(f32[24]{0:T(128)} %param.19) | copy-start | bytes 292
  137.8 2.3 %copy-start.3 = (bf16[768,640]{1,0:T(8,128)(2,1)S(1)}, bf16[768,640]{1,0:T(8,128)(2,1)}, u32[]{:S(2)}) copy-start(bf16[768,640]{1,0:T(8,128)(2,1)} %get-tuple-element.56) | copy-start | bytes 2949124
  140.1 1.6 copy-start.2
  141.2 1.5 copy-start.15
  141.7 2.0 copy-start.14
  142.7 2.1 copy-start.13
  143.7 2.0 copy-start.12
  144.8 2.0 copy-start.11
  145.8 2.0 copy-start.10
  201.1 3.7 %copy-start.19 = (bf16[4,24,512]{2,1,0:T(8,128)(2,1)S(1)}, bf16[4,24,512]{2,1,0:T(8,128)(2,1)}, u32[]{:S(2)}) copy-start(bf16[4,24,512]{2,1,0:T(8,128)(2,1)} %get-tuple-element.68) | copy-start | bytes 294916
  201.1 3.8 %copy-start.18 = (bf16[4,24,640]{2,1,0:T(8,128)(2,1)S(1)}, bf16[4,24,640]{2,1,0:T(8,128)(2,1)}, u32[]{:S(2)}) copy-start(bf16[4,24,640]{2,1,0:T(8,128)(2,1)} %get-tuple-element.69) | copy-start | bytes 368644
  201.1 3.8 %copy-start.17 = (bf16[4,24,640]{2,1,0:T(8,128)(2,1)S(1)}, bf16[4,24,640]{2,1,0:T(8,128)(2,1)}, u32[]{:S(2)}) copy-start(bf16[4,24,640]{2,1,0:T(8,128)(2,1)} %get-tuple-element.70) | copy-start | bytes 368644
  201.1 3.8 %copy-start.16 = (bf16[4,24,640]{2,1,0:T(8,128)(2,1)S(1)}, bf16[4,24,640]{2,1,0:T(8,128)(2,1)}, u32[]{:S(2)}) copy-start(bf16[4,24,640]{2,1,0:T(8,128)(2,1)} %get-tuple-element.71) | copy-start | bytes 368644
  204.9 1.3 copy-start.20

commit v2 on v1

--- a/solution.py
+++ b/solution.py
@@ -42,9 +42,15 @@
     return high, (value - high.astype(jnp.float32)).astype(jnp.bfloat16)
 
 
-def row_loop(total, size, step):
+def run_queue(i, count, queue):
+    for n, item in enumerate(queue):
+        pl.when(i == min(n, count - 1))(item)
+
+
+def row_loop(total, size, step, queue=()):
     def one(i, carry):
         step(pl.multiple_of(i * size, size))
+        run_queue(i, total // size, queue)
         return carry
 
     lax.fori_loop(0, total // size, one, 0)
@@ -73,6 +79,14 @@
     return jnp.where(lane < HD, high, low).astype(jnp.bfloat16)
 
 
+def spans_of(pieces):
+    spans, at = [], 0
+    for piece in pieces:
+        spans.append(slice(at, at + piece.shape[1]))
+        at += piece.shape[1]
+    return spans
+
+
 def stage_norm(r):
     total = r.hidden.shape[0]
 
@@ -84,14 +98,16 @@
 
     row_loop(total, 64, step)
     r.nbt[...] = r.nb[...].T
+
+
+def stage_consts(r):
     r.expand[...] = head_expander(DI)
     r.summer[...] = head_summer(DI)
 
 
 def stage_proj_x(r, k):
     total = r.hidden.shape[0]
-    width = r.wx[k].shape[1]
-    r.raw[8 : 8 + total, k * width : (k + 1) * width] = contract(r.nb[...], r.wx[k][...], 1, 0)
+    r.raw[8 : 8 + total, spans_of(r.wx)[k]] = contract(r.nb[...], r.wx[k][...], 1, 0)
 
 
 def stage_conv(r):
@@ -157,7 +173,7 @@
     )
 
 
-def stage_scan(r):
+def stage_scan(r, queue=()):
     total = r.hidden.shape[0]
     row = lax.broadcasted_iota(jnp.int32, (QLEN, QLEN), 0)
     col = lax.broadcasted_iota(jnp.int32, (QLEN, QLEN), 1)
@@ -193,12 +209,11 @@
                 keys_t, tail, 1, 0
             )
 
-    row_loop(total, QLEN, step)
+    row_loop(total, QLEN, step, queue)
 
 
 def stage_proj_z(r, k):
-    width = r.wz[k].shape[1]
-    r.z[:, k * width : (k + 1) * width] = contract(r.nb[...], r.wz[k][...], 1, 0)
+    r.z[:, spans_of(r.wz)[k]] = contract(r.nb[...], r.wz[k][...], 1, 0)
 
 
 def stage_gate(r):
@@ -286,8 +301,7 @@
 
 
 def stage_grad_z(r, k):
-    width = r.gwz[k].shape[1]
-    part = contract(r.nbt[...], r.dz[:, k * width : (k + 1) * width], 1, 0)
+    part = contract(r.nbt[...], r.dz[:, spans_of(r.gwz)[k]], 1, 0)
     r.gwz[k][...] = part.astype(jnp.bfloat16)
 
 
@@ -304,7 +318,7 @@
     return out
 
 
-def stage_scan_back(r):
+def stage_scan_back(r, queue=()):
     total = r.hidden.shape[0]
     chunks = total // QLEN
     row = lax.broadcasted_iota(jnp.int32, (QLEN, QLEN), 0)
@@ -386,6 +400,10 @@
         d_pre = jnp.where(lane < NH, d_pre, 0.0)
         r.acc_sb[...] += fold(d_pre)
         r.dxb[rows, CONV_CH : CONV_CH + LANES] = d_pre.astype(jnp.bfloat16)
+        rest = r.dxb.shape[1] - CONV_CH - LANES
+        if rest:
+            r.dxb[rows, CONV_CH + LANES :] = jnp.zeros((QLEN, rest), jnp.bfloat16)
+        run_queue(i, chunks, queue)
         return carry
 
     lax.fori_loop(0, chunks, step, 0)
@@ -417,23 +435,18 @@
 
 
 def stage_grad_x(r, k):
-    width = r.gwx[k].shape[1]
-    part = contract(r.nbt[...], r.dxb[:, k * width : (k + 1) * width], 1, 0)
+    part = contract(r.nbt[...], r.dxb[:, spans_of(r.gwx)[k]], 1, 0)
     r.gwx[k][...] = part.astype(jnp.bfloat16)
 
 
-def stage_grad_in(r):
-    total, wide = r.hidden.shape
+def stage_grad_in(r, grads, weights, first):
+    wide = r.hidden.shape[1]
     block = 256
     for at in range(0, wide, block):
-        sums = None
-        for grads, weights in ((r.dz, r.wz), (r.dxb, r.wx)):
-            width = weights[0].shape[1]
-            for k in range(len(weights)):
-                term = contract(
-                    grads[:, k * width : (k + 1) * width], weights[k][at : at + block, :], 1, 1
-                )
-                sums = term if sums is None else sums + term
+        sums = None if first else r.grad_in[:, at : at + block]
+        for span, weight in zip(spans_of(weights), weights):
+            term = contract(grads[:, span], weight[at : at + block, :], 1, 1)
+            sums = term if sums is None else sums + term
         r.grad_in[:, at : at + block] = sums
 
 
@@ -474,9 +487,8 @@
     pass
 
 
-def core_scratch(total, wide):
+def core_scratch(total, wide, span):
     f32, bf16 = jnp.float32, jnp.bfloat16
-    span = CONV_CH + LANES
     return dict(
         nb=((total, wide), bf16),
         nbt=((wide, total), bf16),
@@ -781,6 +793,7 @@
             setattr(r, name, refs[at])
             at += 1
     r.ex = r.z
+    stage_consts(r)
     stage_norm(r)
     for k in range(GROUP):
         stage_proj_x(r, k)
@@ -800,7 +813,8 @@
     stage_conv_back(r)
     for k in range(GROUP):
         stage_grad_x(r, k)
-    stage_grad_in(r)
+    stage_grad_in(r, r.dz, r.wz, True)
+    stage_grad_in(r, r.dxb, r.wx, False)
     stage_norm_back(r)
     stage_vectors(r)
 
@@ -808,7 +822,7 @@
 def run_core(count, hidden, cot, small, wx, wz, wo):
     total, wide = hidden.shape
     f32, bf16 = jnp.float32, jnp.bfloat16
-    scratch = core_scratch(total, wide)
+    scratch = core_scratch(total, wide, sum(w.shape[1] for w in wx))
     vmem = pl.BlockSpec(memory_space=pltpu.VMEM)
     smem = pl.BlockSpec(memory_space=pltpu.SMEM)
     outs = [((total, wide), bf16), ((total, wide), f32), ((8, CONV_CH), f32)]
@@ -898,6 +912,498 @@
     return (block_out, grad_in, g_gain, g_in, g_cw, g_cb, g_sb, g_dl, g_sk, g_mg, g_out)
 
 
+class Plan:
+    def __init__(self, labels):
+        self.labels = labels
+
+    def region(self, ref, free, fixed=()):
+        fixed = dict(fixed)
+        index = []
+        for label in self.labels:
+            if label in fixed:
+                index.append(pl.ds(fixed[label], 1))
+            elif label in free:
+                index.append(slice(None))
+            else:
+                index.append(pl.ds(my_bit(label), 1))
+        return ref.at[tuple(index)]
+
+    def own(self, ref):
+        return ref.at[tuple(my_bit(label) for label in self.labels)]
+
+
+class Spread:
+    def __init__(self, labels, order, ref, sems, stream):
+        self.plan, self.order, self.ref = Plan(labels), order, ref
+        self.sems, self.stream = sems, stream
+
+    def copy(self, step):
+        done = self.order[len(self.order) - step :]
+        label = self.order[len(self.order) - 1 - step]
+        part = self.plan.region(self.ref, done)
+        return pltpu.make_async_remote_copy(
+            src_ref=part,
+            dst_ref=part,
+            send_sem=self.sems[0].at[self.stream, step],
+            recv_sem=self.sems[1].at[self.stream, step],
+            device_id=partner(label),
+            device_id_type=pl.DeviceIdType.MESH,
+        )
+
+    def tick(self, step):
+        if step > 0:
+            self.copy(step - 1).wait_recv()
+        if step < len(self.order):
+            self.copy(step).start()
+
+    def drain(self):
+        for step in range(len(self.order)):
+            self.copy(step).wait_send()
+
+
+class Merge:
+    def __init__(self, labels, order, ref, held, tail, sems, stream):
+        spots = [label for label in labels if label[0] == "rep"]
+        self.plan, self.order, self.ref, self.held = Plan(labels), order, ref, held
+        self.sems, self.stream = sems, stream
+        self.tail = Spread(spots, bits_of("rep"), tail, sems, stream + 1)
+
+    def source(self, step):
+        return self.ref if step == 0 else self.held[step - 1]
+
+    def index(self, step, bit, rest):
+        spots = []
+        for label in self.plan.labels:
+            if label in self.order[:step]:
+                spots.append(0)
+            elif label == self.order[step]:
+                spots.append(bit)
+            else:
+                spots.append(rest[label])
+        return tuple(spots)
+
+    def copy(self, step):
+        label = self.order[step]
+        spots = []
+        for name in self.plan.labels:
+            spots.append(pl.ds(1 - my_bit(name), 1) if name == label else slice(None))
+        return pltpu.make_async_remote_copy(
+            src_ref=self.source(step).at[tuple(spots)],
+            dst_ref=self.held[step],
+            send_sem=self.sems[0].at[self.stream, step],
+            recv_sem=self.sems[1].at[self.stream, step],
+            device_id=partner(label),
+            device_id_type=pl.DeviceIdType.MESH,
+        )
+
+    def add(self, step):
+        label = self.order[step]
+        free = [name for name in self.plan.labels if name not in self.order[: step + 1]]
+        base, target = self.source(step), self.held[step]
+        for number in range(1 << len(free)):
+            rest = {name: (number >> place) % 2 for place, name in enumerate(free)}
+            left = base[self.index(step, my_bit(label), rest)].astype(jnp.float32)
+            spot = self.index(step, 0, rest)
+            total = left + target[spot].astype(jnp.float32)
+            target[spot] = total.astype(target.dtype)
+
+    def tick(self, step):
+        steps = len(self.order)
+        if 0 < step <= steps:
+            self.copy(step - 1).wait_recv()
+            self.add(step - 1)
+        if step < steps:
+            self.copy(step).start()
+            return
+        if step == steps:
+            spot = tuple(0 for _ in self.plan.labels)
+            self.tail.plan.own(self.tail.ref)[...] = self.held[steps - 1][spot]
+        self.tail.tick(step - steps)
+
+    def last(self):
+        return len(self.order) + len(self.tail.order)
+
+    def drain(self):
+        for step in range(len(self.order)):
+            self.copy(step).wait_send()
+        self.tail.drain()
+
+
+class Total:
+    def __init__(self, order, ref, held, sems, stream):
+        self.order, self.ref, self.held = order, ref, held
+        self.sems, self.stream = sems, stream
+
+    def copy(self, step):
+        return pltpu.make_async_remote_copy(
+            src_ref=self.ref if step == 0 else self.held[step - 1],
+            dst_ref=self.held[step],
+            send_sem=self.sems[0].at[self.stream, step],
+            recv_sem=self.sems[1].at[self.stream, step],
+            device_id=partner(self.order[step]),
+            device_id_type=pl.DeviceIdType.MESH,
+        )
+
+    def tick(self, step):
+        if step > 0:
+            self.copy(step - 1).wait_recv()
+            before = self.ref if step == 1 else self.held[step - 2]
+            self.held[step - 1][...] = before[...] + self.held[step - 1][...]
+        if step < len(self.order):
+            self.copy(step).start()
+
+    def drain(self):
+        for step in range(len(self.order)):
+            self.copy(step).wait_send()
+
+
+def side_widths():
+    blocks = -(-(CONV_CH + NH) // (2 * LANES))
+    cuts = [(blocks * k + GROUP - 1) // GROUP for k in range(GROUP + 1)]
+    return [(cuts[k + 1] - cuts[k]) * LANES for k in range(GROUP)]
+
+
+def side_labels():
+    rep = bits_of("rep")
+    return rep[-1:] + bits_of("fsdp") + rep[:-1]
+
+
+def sides(refs):
+    out = []
+    for ref in refs:
+        both = ref.reshape((2, _count(ref.shape[1:-1]), ref.shape[-1]))
+        out += [both.at[0], both.at[1]]
+    return out
+
+
+def flat(ref):
+    return ref.reshape((_count(ref.shape[:-1]), ref.shape[-1]))
+
+
+def _count(shape):
+    count = 1
+    for size in shape:
+        count *= size
+    return count
+
+
+def unpack_small(r, groups):
+    blocks = r.small.reshape((groups, 16, 2 * LANES))
+    size_cw, size_mg, size_gain = (item // groups for item in (CONV_CH, DI, r.hidden.shape[1]))
+    pieces = [blocks[g] for g in range(groups)]
+    r.cw[...] = jnp.concatenate([piece[0:8, :size_cw] for piece in pieces], axis=1)
+    r.mg[...] = jnp.concatenate([piece[5:6, :size_mg] for piece in pieces], axis=1)
+    r.gain[...] = jnp.concatenate([piece[6:7, :size_gain] for piece in pieces], axis=1)
+    r.cb = r.cw.at[4:5, :]
+    r.sb = r.small0.at[8:9, 0:LANES]
+    r.dl = r.small0.at[9:10, 0:LANES]
+    r.sk = r.small0.at[10:11, 0:LANES]
+
+
+def finish_weights(r):
+    rows = r.g_in.shape[0]
+    at = 0
+    for tail in r.tz + r.tx:
+        wide = tail.shape[-1]
+        for side in range(2):
+            value = tail[side].astype(jnp.float32).reshape(rows, wide)
+            stop = min(at + wide, PROJ)
+            r.g_in[:, at:stop] = value[:, : stop - at]
+            at = stop
+    for k in range(GROUP):
+        wide = r.to[k].shape[-1]
+        r.g_out[:, k * wide : (k + 1) * wide] = (
+            r.to[k][...].astype(jnp.float32).reshape(r.g_out.shape[0], wide)
+        )
+
+
+def finish_vectors(r, groups):
+    me = lax.axis_index("fsdp")
+    total = r.vheld[-1][...]
+    full = total.shape[1]
+
+    def mine(first, last, whole, out):
+        count = whole // groups
+        turned = pltpu.roll(total, (full - me * count) % full, 1)
+        out[...] = turned[first:last, :count]
+
+    mine(0, KCONV, CONV_CH, r.g_cw)
+    mine(KCONV, KCONV + 1, CONV_CH, r.g_cb)
+    mine(5, 6, DI, r.g_mg)
+    mine(6, 7, r.hidden.shape[1], r.g_gain)
+    for k, out in enumerate((r.g_sb, r.g_dl, r.g_sk)):
+        out[...] = total[7:8, k * LANES : k * LANES + NH]
+
+
+def fused_kernel(names, *refs):
+    r = Refs()
+    at = 0
+    for name, many in names:
+        if many:
+            setattr(r, name, list(refs[at : at + many]))
+            at += many
+        else:
+            setattr(r, name, refs[at])
+            at += 1
+    r.ex = r.z
+    labels = all_labels()
+    plan = orders()
+    groups = lax.axis_size("fsdp")
+    steps = len(labels)
+    sems = (r.send, r.recv)
+    side_first = side_labels()
+
+    small = Spread(bits_of("fsdp"), bits_of("fsdp"), r.small, sems, 0)
+    xs = [Spread(side_first, plan[k], r.bx[k], sems, 1 + k) for k in range(GROUP)]
+    zs = [Spread(side_first, plan[k], r.bz[k], sems, 1 + GROUP + k) for k in range(GROUP)]
+    os = [Spread(labels, plan[k], r.bo[k], sems, 1 + 2 * GROUP + k) for k in range(GROUP)]
+    base = 1 + 3 * GROUP
+
+    def merges(names_of, refs_of, helds, tails, offset):
+        return [
+            Merge(
+                names_of, plan[k], refs_of[k], helds[k * steps : (k + 1) * steps], tails[k],
+                sems, base + 2 * (offset + k),
+            )
+            for k in range(GROUP)
+        ]
+
+    mo = merges(labels, r.bo, r.ho, r.to, 0)
+    mz = merges(side_first, r.bz, r.hz, r.tz, GROUP)
+    mx = merges(side_first, r.bg, r.hx, r.tx, 2 * GROUP)
+    total = Total(labels[::-1], r.vec, r.vheld, sems, base + 6 * GROUP)
+
+    local = [pltpu.make_async_copy(r.small0, small.plan.own(r.small), r.local.at[0])]
+    side = my_bit(side_first[0])
+    rows = r.bz[0].shape[-2]
+    here = pl.ds(pl.multiple_of(lax.axis_index("rep") // 2 * rows, 16), rows)
+    at = 0
+    for piece in zs + xs:
+        wide = piece.ref.shape[-1]
+        lanes = pl.ds(pl.multiple_of(at + side * wide, LANES), wide)
+        local.append((piece, r.in_rows.at[here, lanes]))
+        at += 2 * wide
+    rows = r.bo[0].shape[-2]
+    here = pl.ds(pl.multiple_of(lax.axis_index("rep") * rows, 16), rows)
+    width = r.bo[0].shape[-1]
+    for k in range(GROUP):
+        local.append((os[k], r.out_rows.at[here, k * width : (k + 1) * width]))
+    for n in range(1, len(local)):
+        piece, source = local[n]
+        local[n] = pltpu.make_async_copy(source, piece.plan.own(piece.ref), r.local.at[n])
+    for copy in local:
+        copy.start()
+    greet(labels)
+    for copy in local:
+        copy.wait()
+
+    def all_tick(pieces, step):
+        for piece in pieces:
+            piece.tick(step)
+
+    r.wx, r.wz, r.gwx = sides(r.bx), sides(r.bz), sides(r.bg)
+    r.wo = [flat(ref) for ref in r.bo]
+    r.gwz, r.gwo = r.wz, r.wo
+
+    fast = len(small.order)
+    small.tick(0)
+    all_tick(xs, 0)
+    stage_consts(r)
+    for step in range(1, fast + 1):
+        small.tick(step)
+        all_tick(xs, step)
+    unpack_small(r, groups)
+    stage_norm(r)
+    for step in range(fast + 1, steps):
+        all_tick(xs, step)
+    all_tick(zs, 0)
+    for k in range(GROUP):
+        xs[k].tick(steps)
+        stage_proj_x(r, 2 * k)
+        stage_proj_x(r, 2 * k + 1)
+    all_tick(zs, 1)
+    stage_conv(r)
+    all_tick(zs, 2)
+    all_tick(os, 0)
+    stage_steps(r)
+    queue = [lambda s=s: all_tick(zs, s) for s in range(3, steps + 1)]
+    queue += [lambda s=s: all_tick(os, s) for s in range(1, 2)]
+    stage_scan(r, queue)
+    for k in range(GROUP):
+        stage_proj_z(r, 2 * k)
+        stage_proj_z(r, 2 * k + 1)
+        if 2 + k < steps:
+            all_tick(os, 2 + k)
+    stage_gate(r)
+    for step in range(2 + GROUP, steps + 1):
+        all_tick(os, step)
+    stage_out(r)
+    for piece in os + zs:
+        piece.drain()
+    for k in range(GROUP):
+        stage_grad_out(r, k)
+        mo[k].tick(0)
+    stage_gate_back(r)
+    all_tick(mo, 1)
+    stage_grad_in(r, r.dz, r.wz, True)
+    for k in range(GROUP):
+        stage_grad_z(r, 2 * k)
+        stage_grad_z(r, 2 * k + 1)
+        mz[k].tick(0)
+    all_tick(mo, 2)
+    queue = []
+
+    def both(s):
+        all_tick(mz, s - 2)
+        all_tick(mo, s)
+
+    for s in range(3, 7):
+        queue.append(lambda s=s: both(s))
+    stage_scan_back(r, queue)
+    last = mx[0].last()
+    both(7)
+    stage_conv_back(r)
+    for k in range(GROUP):
+        stage_grad_x(r, 2 * k)
+        stage_grad_x(r, 2 * k + 1)
+        mx[k].tick(0)
+    all_tick(mz, 6)
+    stage_grad_in(r, r.dxb, r.wx, False)
+    all_tick(mz, 7)
+    all_tick(mx, 1)
+    stage_norm_back(r)
+    stage_vectors(r)
+    total.tick(0)
+    for step in range(2, last + 1):
+        all_tick(mx, step)
+        if step - 1 <= steps:
+            total.tick(step - 1)
+    for step in range(last, steps + 1):
+        total.tick(step)
+    finish_weights(r)
+    finish_vectors(r, groups)
+    small.drain()
+    for piece in xs + mo + mz + mx:
+        piece.drain()
+    total.drain()
+
+
+def run_fused(count, hidden, cot, small0, in_rows, out_rows, in_shard, out_shard):
+    total, wide = hidden.shape
+    f32, bf16 = jnp.float32, jnp.bfloat16
+    groups, reps = lax.axis_size("fsdp"), lax.axis_size("rep")
+    labels, plan = all_labels(), orders()
+    steps = len(labels)
+    widths = side_widths()
+    scratch = core_scratch(total, wide, 2 * sum(widths))
+    nd = (2,) * steps
+    ni, no = in_rows.shape[0] * 2 // reps, out_rows.shape[0] // reps
+    wo = out_rows.shape[1] // GROUP
+    wz = DI // (2 * GROUP)
+    rep_bits = (2,) * len(bits_of("rep"))
+    side_first = side_labels()
+    groups_of = [
+        ("x", ni, widths, side_first), ("z", ni, [wz] * GROUP, side_first),
+        ("o", no, [wo] * GROUP, labels),
+    ]
+    buffers = [("small", [((2,) * len(bits_of("fsdp")) + small0.shape, f32)])]
+    for name, rows, cols, order in groups_of:
+        whole = [(nd + (rows, col), bf16) for col in cols]
+        buffers.append(("b" + name, whole))
+        if name == "x":
+            buffers.append(("bg", whole))
+        held = []
+        for k in range(GROUP):
+            for step in range(steps):
+                gone = plan[k][: step + 1]
+                kept = tuple(1 if n in gone else 2 for n in order)
+                held.append((kept + (rows, cols[k]), bf16))
+        buffers.append(("h" + name, held))
+        buffers.append(("t" + name, [(rep_bits + (rows, col), bf16) for col in cols]))
+    buffers.append(("vec", [((8, CONV_CH), f32)]))
+    buffers.append(("vheld", [((8, CONV_CH), f32)] * steps))
+    buffers.append(("cw", [((8, CONV_CH), f32)]))
+    buffers.append(("mg", [((1, DI), f32)]))
+    buffers.append(("gain", [((1, wide), f32)]))
+    buffers += [(name, [item]) for name, item in scratch.items()]
+    outs = [
+        ("block_out", (total, wide), bf16),
+        ("grad_in", (total, wide), f32),
+        ("g_gain", (1, wide // groups), f32),
+        ("g_in", in_shard, f32),
+        ("g_cw", (KCONV, CONV_CH // groups), f32),
+        ("g_cb", (1, CONV_CH // groups), f32),
+        ("g_sb", (1, NH), f32),
+        ("g_dl", (1, NH), f32),
+        ("g_sk", (1, NH), f32),
+        ("g_mg", (1, DI // groups), f32),
+        ("g_out", out_shard, f32),
+    ]
+    names = [(n, 0) for n in ("count", "hidden", "cot", "small0", "in_rows", "out_rows")]
+    names += [(out[0], 0) for out in outs]
+    single = ("small", "vec", "cw", "mg", "gain") + tuple(scratch)
+    shapes = []
+    for name, items in buffers:
+        names.append((name, 0 if name in single else len(items)))
+        shapes += [pltpu.VMEM(*item) for item in items]
+    names += [("send", 0), ("recv", 0), ("local", 0)]
+    streams = 2 + 9 * GROUP
+    slots = pltpu.SemaphoreType.DMA((streams, steps))
+    shapes += [slots, slots, pltpu.SemaphoreType.DMA((1 + 3 * GROUP,))]
+    vmem = pl.BlockSpec(memory_space=pltpu.VMEM)
+    smem = pl.BlockSpec(memory_space=pltpu.SMEM)
+    return pl.pallas_call(
+        functools.partial(fused_kernel, names),
+        in_specs=[smem] + [vmem] * 5,
+        out_specs=[vmem] * len(outs),
+        out_shape=[jax.ShapeDtypeStruct(*out[1:]) for out in outs],
+        scratch_shapes=shapes,
+        compiler_params=pltpu.CompilerParams(
+            collective_id=2, has_side_effects=True, vmem_limit_bytes=67043328
+        ),
+        name="fused_block",
+    )(count, hidden, cot, small0, in_rows, out_rows)
+
+
+def fused_body(
+    hidden_in, cotangent, lengths, norm_gain, in_weight, conv_weight, conv_bias,
+    step_bias, decay_log, skip_weight, mix_gain, out_weight,
+):
+    small0 = jnp.zeros((16, 2 * LANES), jnp.float32)
+    rows = [conv_weight, conv_bias[None], mix_gain[None], norm_gain[None], norm_gain[None, :0]]
+    rows += [step_bias[None], decay_log[None], skip_weight[None]]
+    at = 0
+    for row in rows:
+        high, wide = row.shape
+        row = row.astype(jnp.float32)
+        small0 = small0 + jnp.pad(row, ((at, 16 - high - at), (0, 2 * LANES - wide)))
+        at += high
+    full = DI + 2 * sum(side_widths())
+    in_rows = jnp.pad(in_weight, ((0, 0), (0, full - in_weight.shape[1])))
+    outs = run_fused(
+        lengths, hidden_in, cotangent, small0, in_rows, out_weight,
+        in_weight.shape, out_weight.shape,
+    )
+    outs = list(outs)
+    for n in (2, 5, 6, 7, 8, 9):
+        outs[n] = outs[n].reshape(-1)
+    return tuple(outs)
+
+
+def pick_body(
+    hidden_in, cotangent, lengths, norm_gain, in_weight, conv_weight, conv_bias,
+    step_bias, decay_log, skip_weight, mix_gain, out_weight,
+):
+    reps = lax.axis_size("rep")
+    whole = in_weight.shape[0] % (8 * reps) == 0 and out_weight.shape[0] % (16 * reps) == 0
+    whole = whole and reps > 1
+    chosen = fused_body if whole and conv_bias.shape[0] <= 2 * LANES else body
+    return chosen(
+        hidden_in, cotangent, lengths, norm_gain, in_weight, conv_weight, conv_bias,
+        step_bias, decay_log, skip_weight, mix_gain, out_weight,
+    )
+
+
 def solution(mesh):
     in_specs = (
         P(("fsdp", "rep"), None),
@@ -926,4 +1432,4 @@
         P("fsdp"),
         P("fsdp", None),
     )
-    return jax.shard_map(body, mesh=mesh, in_specs=in_specs, out_specs=out_specs, check_vma=False)
+    return jax.shard_map(pick_body, mesh=mesh, in_specs=in_specs, out_specs=out_specs, check_vma=False)

time: 210 us -> 168 us (0.80)
  local copies, waits for them, and re-layouts: 39.8 us -> 12.5 us
  Pallas kernels: 165 us -> 152 us
    reshape x22 -> x0, local copies, waits for them, and re-layouts: 23.1 us -> none  [the longest x9 10.4 us: to_order(): split = array.reshape((2,) * len(labels) + (rows, array.shape[1]))]
    pallas_call x3 -> x1, Pallas kernels: 165 us -> 152 us  [run_fused(): pl.pallas_call(functools.partial(fused_kernel, names), in_specs=[smem] +...]
    unnamed x54 -> x31, local copies, waits for them, and re-layouts: 3.76 us -> 9.19 us
    broadcast_in_dim x3 -> x0, local copies, waits for them, and re-layouts: 4.19 us -> none  [the longest x2 2.79 us: body(): pieces = [whole_lanes(in_rows[:, cut])[None] for cut in x_cuts + z_cuts]]
    convert_element_type x6 -> x0, other arithmetic: 3.28 us -> none  [the longest x1 1.9 us: body(): g_out = jnp.concatenate(sums[6:], axis=1).astype(f32)]
    dynamic_slice x4 -> x0, local copies, waits for them, and re-layouts: 2.52 us -> none  [mine(): return lax.dynamic_slice_in_dim(array, me * count, count, array.ndim - 1)]
    concatenate x2 -> x0, local copies, waits for them, and re-layouts: 2.11 us -> none  [the longest x1 2.09 us: body(): jnp.concatenate([norm_gain, conv_weight.reshape(-1), conv_bias, mix_gain])]
where the time goes in v2:
time: 168 us; the launch traced here: 167 us
  Pallas kernels  152 us (90%)
  local copies, waits for them, and re-layouts  12.5 us (7%)
    pallas_call x1, Pallas kernels, run_fused(): pl.pallas_call(functools.partial(fused_kernel, names), in_specs=[smem] +...  152 us
    unnamed x31, local copies, waits for them, and re-layouts  9.19 us

profile of v2, /device:TPU:0, one launch (start us, length us, event | category | flops | bytes accessed | tf_op | source)
XLA Modules:
  0.0 167.4 jit_solution(10171619583358375972)
XLA Ops:
  1.3 0.7 convert_element_type.31
  1.9 0.7 convert_element_type.32
  2.6 1.4 pad_add_fusion.refs_3_
  4.0 2.0 %pad.57.refs_4_ = bf16[96,3584]{1,0:T(8,128)(2,1)} pad(bf16[96,3352]{1,0:T(8,128)(2,1)} %param.16, bf16[]{:T(256)} %constant.5.clone.1), padding=0_0x0_232 | pad | bytes 1331714 | tf_op jit(solution)/shard_map/jit(_pad)/pad | solution.py:1382
  6.0 152.2 %fused_block.1 = (bf16[512,768]{1,0:T(8,128)(2,1)}, f32[512,768]{1,0:T(8,128)}, f32[1,96]{1,0:T(1,128)}, f32[96,3352]{1,0:T(8,128)}, f32[4,224]{1,0:T(4,128)}, /...) custom-call(s32[1]{0:T(128)S(6)} %copy.34.refs_0_, ...), custom_call_target="tpu_custom_call" | custom-call | tf_op jit(solution)/shard_map/fused_block/pallas_call | solution.py:1355
  158.2 0.0 copy-start
  158.2 2.2 %copy.35 = bf16[512,768]{1,0:T(8,128)(2,1)} copy(bf16[512,768]{1,0:T(8,128)(2,1)} %get-tuple-element.44) | data formatting | bytes 1572864
  160.4 0.0 copy-done
  160.4 0.0 copy-start.9
  160.4 1.1 copy.36
  161.5 0.0 copy-done.9
  161.6 0.0 copy-start.7
  161.6 0.0 copy-start.6
  161.6 0.0 copy-start.4
  161.6 0.0 copy-start.2
  161.6 0.5 copy.37
  162.1 0.2 copy-done.1
  162.3 1.1 copy.38
  163.4 0.0 copy-done.3
  163.4 0.6 copy.39
  164.0 0.0 copy-done.5
  164.0 0.6 copy.40
  164.5 0.0 copy-done.8
  164.5 0.5 copy.41
  165.0 0.0 copy-done.7
  165.0 0.5 copy.42
  165.5 0.0 copy-done.6
  165.6 0.5 copy.43
  166.1 0.0 copy-done.4
  166.1 0.6 copy.44
  166.6 0.0 copy-done.2
  166.6 0.8 copy.45
  (4 shorter events, 0.0 us)
Async XLA Ops:
  158.2 2.2 %copy-start = (f32[512,768]{1,0:T(8,128)S(1)}, f32[512,768]{1,0:T(8,128)}, u32[]{:S(2)}) copy-start(f32[512,768]{1,0:T(8,128)} %get-tuple-element.45) | copy-start | bytes 4718596
  160.4 1.1 copy-start.9
  160.4 1.9 %copy-start.1 = (f32[96,3352]{1,0:T(8,128)S(1)}, f32[96,3352]{1,0:T(8,128)}, u32[]{:S(2)}) copy-start(f32[96,3352]{1,0:T(8,128)} %get-tuple-element.47) | copy-start | bytes 3861508
  161.5 1.8 %copy-start.3 = (f32[4,224]{1,0:T(4,128)S(1)}, f32[4,224]{1,0:T(4,128)}, u32[]{:S(2)}) copy-start(f32[4,224]{1,0:T(4,128)} %get-tuple-element.48) | copy-start | bytes 10756
  161.6 2.4 %copy-start.5 = (f32[1,224]{1,0:T(1,128)S(1)}, f32[1,224]{1,0:T(1,128)}, u32[]{:S(2)}) copy-start(f32[1,224]{1,0:T(1,128)} %get-tuple-element.27) | copy-start | bytes 2692
  161.6 3.0 %copy-start.8 = (f32[1,24]{1,0:T(1,128)S(1)}, f32[1,24]{1,0:T(1,128)}, u32[]{:S(2)}) copy-start(f32[1,24]{1,0:T(1,128)} %get-tuple-element.28) | copy-start | bytes 292
  161.6 3.5 %copy-start.7 = (f32[1,24]{1,0:T(1,128)S(1)}, f32[1,24]{1,0:T(1,128)}, u32[]{:S(2)}) copy-start(f32[1,24]{1,0:T(1,128)} %get-tuple-element.29) | copy-start | bytes 292
  161.6 4.0 %copy-start.6 = (f32[1,24]{1,0:T(1,128)S(1)}, f32[1,24]{1,0:T(1,128)}, u32[]{:S(2)}) copy-start(f32[1,24]{1,0:T(1,128)} %get-tuple-element.30) | copy-start | bytes 292
  161.6 4.5 %copy-start.4 = (f32[1,192]{1,0:T(1,128)S(1)}, f32[1,192]{1,0:T(1,128)}, u32[]{:S(2)}) copy-start(f32[1,192]{1,0:T(1,128)} %get-tuple-element.31) | copy-start | bytes 2308
  161.6 5.0 %copy-start.2 = (f32[192,768]{1,0:T(8,128)S(1)}, f32[192,768]{1,0:T(8,128)}, u32[]{:S(2)}) copy-start(f32[192,768]{1,0:T(8,128)} %get-tuple-element.54) | copy-start | bytes 1769476
